TPU v7x, 128 devices: a whole 4x4x4 slice. The times are simulated.
128 devices in a mesh: tm: 4 (over y), region: 32 (over z, x, core).
Axes of the slice: x: 4, y: 4, z: 4, core: 2. Of those that a mesh axis runs over, the one named last changes fastest.
Arguments:
- search_one: float32 [4, 548, 32768], P('tm', None, 'region'), may hold values from -6 to 6
- search_two: float32 [4, 548, 32768], P('tm', None, 'region'), may hold values from -6 to 6
- column_gain: float32 [4, 548, 32768], P('tm', None, 'region'), may hold values from 0.5 to 1.25
- model_matrix: float32 [4, 548, 548], P('tm'), may hold values from -0.25 to 0.25
- obs_owner: int32 [4, 32768], P('tm', 'region'), may hold values from 0 to 31, as said below
- observe_matrix: float32 [4, 32, 548, 1024], P('tm', 'region'), may hold values from -0.25 to 0.25
- error_weight: float32 [4, 32, 1024], P('tm', 'region'), may hold values from 0.25 to 4
- channel_mask: int32 [4, 32, 1024], P('tm', 'region'), may hold values 0 or 1
Outputs:
- forward_state: float32 [4, 548, 32768], P('tm', None, 'region')
- gradient: float32 [4, 548, 32768], P('tm', None, 'region')
Inputs may be any that keep to these rules, and one draw needn't show every extreme that they name: `obs_owner`: among the 1024 columns of one device (one subwindow, one aligned block of 1024 columns) no owner appears more than 48 times; in every subwindow one owner appears exactly 48 times in every block.
All inputs are finite; a program needn't handle non-finite values. No bound on the sum of `channel_mask` on one device may be relied on, other than what follows from the above.
Results may differ from a plain program's by a relative error of at most 0.0003.
Values sent between devices are 32-bit elements; how exact they have to be, the bound alone decides.
A program may use at most 128 MiB of HBM per device.

v0:
```python
import jax
import jax.numpy as jnp
from jax import lax
from jax.experimental import pallas as pl
from jax.experimental.pallas import tpu as pltpu
from jax.sharding import PartitionSpec as P

F32 = jnp.float32
BF16 = jnp.bfloat16
MESH = pl.DeviceIdType.MESH

OFFDIAG = ((0, 1), (0, 2), (0, 3), (1, 2), (1, 3), (2, 3))
FOLD_AT = 768
TAIL_AT = 1024
TAIL = 40
PACKED = TAIL_AT + 5 * TAIL
HALVES = ((0, 616, 312), (616, 608, 304))
SLOT = 64
CHUNK = 128


def split(x):
    high = x.astype(BF16)
    return high, (x - high.astype(F32)).astype(BF16)


def dot(a, b):
    return jnp.dot(a, b, preferred_element_type=F32)


def dot_nt(a, b):
    return lax.dot_general(a, b, (((1,), (1,)), ((), ())), preferred_element_type=F32)


def pack_kernel(matrix_ref, error_ref, mask_ref, out_ref):
    weight = error_ref[...] * mask_ref[...].astype(F32)
    matrix = matrix_ref[...]
    high, low = split(matrix)
    whigh, wlow = split(matrix * weight)

    def product(r0, r1, c0, c1):
        a, b = slice(r0, r1), slice(c0, c1)
        return dot_nt(whigh[a], high[b]) + (dot_nt(whigh[a], low[b]) + dot_nt(wlow[a], high[b]))

    top = product(0, 256, 0, 512)
    mid = product(256, 512, 256, 512)
    nv = matrix.shape[0]
    tail = product(512, nv, 0, nv)

    def block(i, j):
        if i < 2:
            return top[128 * i : 128 * i + 128, 128 * j : 128 * j + 128]
        return mid[128 * i - 256 : 128 * i - 128, 128 * j - 256 : 128 * j - 128]

    for at, (i, j) in enumerate(OFFDIAG):
        out_ref[128 * at : 128 * at + 128, :] = block(i, j)
    row = lax.broadcasted_iota(jnp.int32, (128, 128), 0)
    col = lax.broadcasted_iota(jnp.int32, (128, 128), 1)
    for pair in range(2):
        upper, lower = block(2 * pair, 2 * pair), block(2 * pair + 1, 2 * pair + 1)
        at = FOLD_AT + 128 * pair
        out_ref[at : at + 128, :] = jnp.where(row <= col, upper, lower)
    rest = nv - 512
    for j in range(5):
        at = TAIL_AT + TAIL * j
        if j < 4:
            out_ref[at : at + rest, :] = tail[:, 128 * j : 128 * j + 128]
            if j % 2 == 1:
                line = jnp.sum(jnp.where(row == col, block(j, j), 0.0), axis=0, keepdims=True)
            else:
                line = jnp.zeros((1, 128), F32)
            out_ref[at + rest : at + TAIL, :] = jnp.broadcast_to(line, (TAIL - rest, 128))
        else:
            out_ref[at : at + TAIL, :] = jnp.zeros((TAIL, 128), F32)
            out_ref[at : at + rest, 0:rest] = tail[:, 512:nv]


def pack(jacobian, error, mask):
    return pl.pallas_call(
        pack_kernel,
        out_shape=jax.ShapeDtypeStruct((PACKED, 128), F32),
        name="pack",
    )(jacobian, error, mask)


def sweep_kernel(
    one_ref, two_ref, gain_ref, matrix_ref, turned_ref, packed_ref,
    forward_ref, swept_ref, gathered_ref,
    into_f, into_b, out_b, m_high, m_low, t_high, t_low,
    f_send, f_recv, b_send, b_recv, g_send, g_recv, p_send, p_recv, own_sem,
):
    k = lax.axis_index("tm")
    region = lax.axis_index("region")
    core = region % 2
    x = (region // 2) % 4
    z = region // 8
    chunks = into_f.shape[0]

    def chip(dz, dx):
        return ((z + dz + 4) % 4 * 4 + (x + dx + 4) % 4) * 2 + core

    partner = region + 1 - 2 * core
    barrier = pltpu.get_barrier_semaphore()
    around = [(k, chip(1, 0)), (k, chip(-1, 0)), (k, chip(0, 1)), (k, chip(0, -1)), (k, partner),
              ((k + 1) % 4, region), ((k + 3) % 4, region)]
    for who in around:
        pl.semaphore_signal(barrier, inc=1, device_id=who, device_id_type=MESH)
    pl.semaphore_wait(barrier, len(around))

    def columns(c):
        return pl.ds(pl.multiple_of(c * CHUNK, CHUNK), CHUNK)

    def send_f(src, c):
        return pltpu.make_async_remote_copy(
            src_ref=src, dst_ref=into_f.at[c], send_sem=f_send.at[c], recv_sem=f_recv.at[c],
            device_id=((k + 1) % 4, region), device_id_type=MESH,
        )

    def send_b(c):
        return pltpu.make_async_remote_copy(
            src_ref=out_b.at[c], dst_ref=into_b.at[c], send_sem=b_send.at[c], recv_sem=b_recv.at[c],
            device_id=((k + 3) % 4, region), device_id_type=MESH,
        )

    def step_to(primary, by):
        return chip(by, 0) if primary == "z" else chip(0, by)

    def block_at(half, dp, dq):
        if half == 0:
            return chip(dq, dp)
        return chip(dp, dq)

    axes = (("x", "z"), ("z", "x"))
    sends = []

    def relay(half, dp, dq, piece, axis, by):
        start, size, cut = HALVES[half]
        if piece == 0:
            start, size = start, cut
        elif piece == 1:
            start, size = start + cut, size - cut
        block = block_at(half, dp, dq)
        own = dp == 0 and dq == 0
        rows = pl.ds(start, size)
        number = len(sends)
        rp, rq = dp % 4, dq % 4
        if axis == axes[half][0]:
            rp = (dp - by) % 4
        else:
            rq = (dq - by) % 4
        copy = pltpu.make_async_remote_copy(
            src_ref=packed_ref.at[rows] if own else gathered_ref.at[block, rows],
            dst_ref=gathered_ref.at[block, rows],
            send_sem=g_send.at[number],
            recv_sem=g_recv.at[half, rp * 4 + rq, 1 if piece == 1 else 0],
            device_id=(k, step_to(axis, by)),
            device_id_type=MESH,
        )
        copy.start()
        sends.append(copy)

    def arrived(half, dp, dq, piece):
        start, size, cut = HALVES[half]
        if piece == 0:
            start, size = start, cut
        elif piece == 1:
            start, size = start + cut, size - cut
        block = block_at(half, dp, dq)
        ref = gathered_ref.at[block, pl.ds(start, size)]
        sem = g_recv.at[half, dp % 4 * 4 + dq % 4, 1 if piece == 1 else 0]
        pltpu.make_async_copy(ref, ref, sem).wait()

    shared = []

    def share(half, dp, dq):
        start, size, _ = HALVES[half]
        block = block_at(half, dp, dq)
        rows = pl.ds(start, size)
        own = dp == 0 and dq == 0
        at = dp % 4 * 4 + dq % 4
        copy = pltpu.make_async_remote_copy(
            src_ref=packed_ref.at[rows] if own else gathered_ref.at[block, rows],
            dst_ref=gathered_ref.at[block, rows],
            send_sem=p_send.at[half, at],
            recv_sem=p_recv.at[half, at],
            device_id=(k, partner),
            device_id_type=MESH,
        )
        copy.start()
        shared.append((half, dp, dq, copy))

    def first(half, by):
        main, other = axes[half]
        arrived(half, by, 0, None)
        relay(half, by, 0, 0 if by == -1 else 1, main, -by)
        relay(half, by, 0, None, other, 1)
        relay(half, by, 0, None, other, -1)
        share(half, by, 0)

    def opposite(half):
        _, other = axes[half]
        arrived(half, 2, 0, 0)
        arrived(half, 2, 0, 1)
        relay(half, 2, 0, None, other, 1)
        relay(half, 2, 0, None, other, -1)
        share(half, 2, 0)

    def second(half, dp, by):
        _, other = axes[half]
        arrived(half, dp, by, None)
        relay(half, dp, by, 0 if by == -1 else 1, other, -by)
        share(half, dp, by)

    def last(half, dp):
        arrived(half, dp, 2, 0)
        arrived(half, dp, 2, 1)
        share(half, dp, 2)

    for half in range(2):
        main, _ = axes[half]
        relay(half, 0, 0, None, main, 1)
        relay(half, 0, 0, None, main, -1)
    for half in range(2):
        _, other = axes[half]
        relay(half, 0, 0, None, other, 1)
        relay(half, 0, 0, None, other, -1)

    @pl.when(k == 0)
    def _():
        for c in range(chunks):
            send_f(one_ref.at[:, c * CHUNK : (c + 1) * CHUNK], c).start()

    for half in range(2):
        share(half, 0, 0)
    own_copy = pltpu.make_async_copy(packed_ref, gathered_ref.at[region], own_sem)
    own_copy.start()

    high, low = split(matrix_ref[...])
    m_high[...], m_low[...] = high, low
    high, low = split(turned_ref[...])
    t_high[...], t_low[...] = high, low

    def times(a_high, a_low, v):
        v_high, v_low = split(v)
        both = dot(a_high[...], jnp.concatenate([v_high, v_low], axis=1))
        return both[:, :CHUNK] + (both[:, CHUNK:] + dot(a_low[...], v_high))

    events = {
        1: [(first, 0, -1), (first, 1, -1), (first, 0, 1), (first, 1, 1)],
        3: [(second, 0, 0, -1), (second, 1, 0, -1), (second, 0, 0, 1), (second, 1, 0, 1)],
        4: [(opposite, 0), (opposite, 1)],
        5: [(second, 0, -1, -1), (second, 1, -1, -1), (second, 0, -1, 1), (second, 1, -1, 1)],
        6: [(second, 0, 1, -1), (second, 1, 1, -1), (second, 0, 1, 1), (second, 1, 1, 1)],
        7: [(last, 0, 0), (last, 1, 0)],
        8: [(second, 0, 2, -1), (second, 1, 2, -1), (second, 0, 2, 1), (second, 1, 2, 1)],
        9: [(last, 0, -1), (last, 1, -1), (last, 0, 1), (last, 1, 1)],
        10: [(last, 0, 2), (last, 1, 2)],
    }

    def tick(t, carry):
        cb = t - (3 - k)

        @pl.when((cb >= 0) & (cb < chunks))
        def _():
            @pl.when(k < 3)
            def _():
                send_b(cb).wait_recv()
                swept_ref[:, columns(cb)] = two_ref[:, columns(cb)] + into_b[cb]

            @pl.when(k == 3)
            def _():
                swept_ref[:, columns(cb)] = two_ref[:, columns(cb)]

            @pl.when(k > 0)
            def _():
                out_b[cb] = times(t_high, t_low, gain_ref[:, columns(cb)] * swept_ref[:, columns(cb)])
                send_b(cb).start()

        cf = t - k

        @pl.when((cf >= 0) & (cf < chunks) & (k > 0))
        def _():
            send_f(into_f.at[cf], cf).wait_recv()
            forward_ref[:, columns(cf)] = one_ref[:, columns(cf)] + gain_ref[:, columns(cf)] * times(
                m_high, m_low, into_f[cf]
            )

            @pl.when(k < 3)
            def _():
                send_f(forward_ref.at[:, columns(cf)], cf).start()

        return carry

    at = 0
    for tick_end in sorted(events):
        lax.fori_loop(at, tick_end + 1, tick, 0)
        at = tick_end + 1
        for event in events[tick_end]:
            event[0](*event[1:])
    lax.fori_loop(at, chunks + 3, tick, 0)

    @pl.when(k == 0)
    def _():
        forward_ref[...] = one_ref[...]

    @pl.when(k < 3)
    def _():
        for c in range(chunks):
            send_f(into_f.at[c], c).wait_send()

    @pl.when(k > 0)
    def _():
        for c in range(chunks):
            send_b(c).wait_send()

    own_copy.wait()
    for copy in sends:
        copy.wait_send()
    for half, dp, dq, copy in shared:
        copy.wait_send()
        start, size, _ = HALVES[half]
        block = block_at(half, dp, dq) + 1 - 2 * core
        ref = gathered_ref.at[block, pl.ds(start, size)]
        pltpu.make_async_copy(ref, ref, p_recv.at[half, dp % 4 * 4 + dq % 4]).wait()


def sweep(one, two, gain, matrix, turned, packed):
    rows, cols = one.shape
    chunks = cols // CHUNK
    vmem = pl.BlockSpec(memory_space=pltpu.VMEM)
    return pl.pallas_call(
        sweep_kernel,
        out_shape=(
            jax.ShapeDtypeStruct((rows, cols), F32),
            jax.ShapeDtypeStruct((rows, cols), F32),
            jax.ShapeDtypeStruct((32, PACKED, 128), F32),
        ),
        in_specs=[vmem] * 6,
        out_specs=(vmem, vmem, pl.BlockSpec(memory_space=pl.ANY)),
        scratch_shapes=[
            pltpu.VMEM((chunks, rows, CHUNK), F32),
            pltpu.VMEM((chunks, rows, CHUNK), F32),
            pltpu.VMEM((chunks, rows, CHUNK), F32),
            pltpu.VMEM((rows, rows), BF16),
            pltpu.VMEM((rows, rows), BF16),
            pltpu.VMEM((rows, rows), BF16),
            pltpu.VMEM((rows, rows), BF16),
            pltpu.SemaphoreType.DMA((chunks,)),
            pltpu.SemaphoreType.DMA((chunks,)),
            pltpu.SemaphoreType.DMA((chunks,)),
            pltpu.SemaphoreType.DMA((chunks,)),
            pltpu.SemaphoreType.DMA((40,)),
            pltpu.SemaphoreType.DMA((2, 16, 2)),
            pltpu.SemaphoreType.DMA((2, 16)),
            pltpu.SemaphoreType.DMA((2, 16)),
            pltpu.SemaphoreType.DMA,
        ],
        compiler_params=pltpu.CompilerParams(
            collective_id=0, has_side_effects=True, vmem_limit_bytes=60 * 1024 * 1024
        ),
        name="sweep",
    )(one, two, gain, matrix, turned, packed)


def apply_kernel(
    owner_ref, forward_ref, swept_ref, gathered_ref,
    state_ref, gradient_ref,
    x_high, x_low, slot_row, slot_col, full, right,
):
    step = pl.program_id(0)
    rows, cols = forward_ref.shape
    pad = full.shape[1] // 2

    @pl.when(step == 0)
    def _():
        owner = owner_ref[...]
        onehot = (owner == lax.broadcasted_iota(jnp.int32, (32, cols), 0)).astype(F32)
        earlier = (
            lax.broadcasted_iota(jnp.int32, (cols, cols), 0) < lax.broadcasted_iota(jnp.int32, (cols, cols), 1)
        ).astype(F32)
        before = dot(onehot.astype(BF16), earlier.astype(BF16))
        placed = jnp.sum(before * onehot, axis=0, keepdims=True)
        slot = owner.astype(F32) * SLOT + placed
        slot_row[...] = jnp.broadcast_to(slot, slot_row.shape)
        slot_col[...] = jnp.broadcast_to(slot, (128, cols)).T
        high, low = split(forward_ref[...])
        x_high[...], x_low[...] = high, low
        state_ref[...] = forward_ref[...]
        gradient_ref[...] = swept_ref[...]
        right[...] = jnp.zeros_like(right)
        full[...] = jnp.zeros_like(full)

    wide = 4 * SLOT
    base = (step * wide).astype(F32)
    lane = lax.broadcasted_iota(jnp.int32, (cols, 128), 1).astype(F32) + base
    pick = jnp.concatenate(
        [(slot_col[...] == lane).astype(BF16), (slot_col[...] == lane + 128.0).astype(BF16)], axis=1
    )
    line = lax.broadcasted_iota(jnp.int32, (wide, cols), 0).astype(F32) + base
    place = (jnp.broadcast_to(slot_row[0:1, :], (wide, cols)) == line).astype(BF16)
    s_high = dot(x_high[...], pick)
    s_low = dot(x_low[...], pick)

    row = lax.broadcasted_iota(jnp.int32, (128, 128), 0)
    col = lax.broadcasted_iota(jnp.int32, (128, 128), 1)
    left_lanes = lax.broadcasted_iota(jnp.int32, (rows, 128), 1) < SLOT
    rest = rows - 512

    def put(at_row, at_col, value):
        high, low = split(value)
        r, c = value.shape
        full[at_row : at_row + r, at_col : at_col + c] = high
        full[at_row : at_row + r, pad + at_col : pad + at_col + c] = low

    answers = []
    for pair in range(2):
        lanes = slice(128 * pair, 128 * pair + 128)
        high = s_high[:, lanes]
        low = pltpu.roll(s_low[:, lanes], SLOT, 1)
        outs = []
        for side in range(2):
            mine = left_lanes if side == 0 else jnp.logical_not(left_lanes)
            right[0:rows, :] = jnp.where(mine, high, low).astype(BF16)
            right[pad : pad + rows, :] = jnp.where(mine, high, 0.0).astype(BF16)
            g = gathered_ref.at[2 * pair + side]
            for at, (i, j) in enumerate(OFFDIAG):
                value = g[128 * at : 128 * at + 128, :]
                put(128 * i, 128 * j, value)
                put(128 * j, 128 * i, value.T)
            for fold in range(2):
                at = FOLD_AT + 128 * fold
                value = g[at : at + 128, :]
                turned = value.T
                put(256 * fold, 256 * fold, jnp.where(row <= col, value, turned))
                line_at = TAIL_AT + TAIL * (2 * fold + 1) + rest
                diagonal = jnp.broadcast_to(g[line_at : line_at + 1, :], (128, 128))
                lower = jnp.where(row > col, value, jnp.where(row < col, turned, diagonal))
                put(256 * fold + 128, 256 * fold + 128, lower)
            for j in range(5):
                at = TAIL_AT + TAIL * j
                value = g[at : at + rest, :]
                put(512, 128 * j, value)
                if j < 4:
                    tall = jnp.concatenate([value, jnp.zeros((128 - rest, 128), F32)], axis=0)
                    put(128 * j, 512, tall.T)
            outs.append(dot(full[...], right[...]))
        even, odd = outs
        answers.append(
            jnp.where(left_lanes, even + pltpu.roll(even, SLOT, 1), odd + pltpu.roll(odd, SLOT, 1))
        )
    high, low = split(jnp.concatenate(answers, axis=1))
    gradient_ref[...] += dot(high, place) + dot(low, place)


def apply(owner, forward, swept, gathered):
    rows, cols = forward.shape
    whole = pl.BlockSpec((rows, cols), lambda i: (0, 0))
    pad = 640
    return pl.pallas_call(
        apply_kernel,
        grid=(8,),
        out_shape=(jax.ShapeDtypeStruct((rows, cols), F32), jax.ShapeDtypeStruct((rows, cols), F32)),
        in_specs=[
            pl.BlockSpec((1, cols), lambda i: (0, 0)),
            whole,
            whole,
            pl.BlockSpec((4, PACKED, 128), lambda i: (i, 0, 0)),
        ],
        out_specs=(whole, whole),
        scratch_shapes=[
            pltpu.VMEM((rows, cols), BF16),
            pltpu.VMEM((rows, cols), BF16),
            pltpu.VMEM((8, cols), F32),
            pltpu.VMEM((cols, 128), F32),
            pltpu.VMEM((rows, 2 * pad), BF16),
            pltpu.VMEM((2 * pad, 128), BF16),
        ],
        compiler_params=pltpu.CompilerParams(vmem_limit_bytes=60 * 1024 * 1024),
        name="apply",
    )(owner, forward, swept, gathered)


def body(search_one, search_two, column_gain, model_matrix, obs_owner, observe_matrix, error_weight, channel_mask):
    packed = pack(observe_matrix[0, 0], error_weight[0], channel_mask[0])
    forward, swept, gathered = sweep(
        search_one[0], search_two[0], column_gain[0], model_matrix[0], model_matrix[0].T, packed
    )
    state, gradient = apply(obs_owner, forward, swept, gathered)
    return state[None], gradient[None]


def solution(mesh):
    return jax.shard_map(
        body,
        mesh=mesh,
        in_specs=(
            P("tm", None, "region"),
            P("tm", None, "region"),
            P("tm", None, "region"),
            P("tm", None, None),
            P("tm", "region"),
            P("tm", "region", None, None),
            P("tm", "region", None),
            P("tm", "region", None),
        ),
        out_specs=(P("tm", None, "region"), P("tm", None, "region")),
        check_vma=False,
    )
```

profile of v0, /device:TPU:1, one launch (start us, length us, event | category | flops | bytes accessed | tf_op | source)
XLA Modules:
  0.0 150.6 jit_solution(1358722512197684143)
XLA Ops:
  0.6 0.0 copy-start
  0.6 2.6 %copy.26 = f32[1,548,548]{2,1,0:T(8,128)} copy(f32[1,548,548]{2,0,1:T(1,128)} %param.11) | data formatting | bytes 2402432 | tf_op jit(solution)/shard_map/squeeze | solution.py:486
  3.3 0.0 copy-done
  3.3 2.8 %copy.10 = f32[1,548,548]{1,2,0:T(8,128)} copy(f32[1,548,548]{2,0,1:T(1,128)S(1)} %copy-done) | data formatting | bytes 2402432 | tf_op args[3]
  6.0 0.0 copy-start.2
  6.0 3.7 %copy.25 = f32[1,548,1024]{2,1,0:T(8,128)} copy(f32[1,548,1024]{2,0,1:T(1,128)} %param.8) | data formatting | bytes 4489216
  9.8 0.0 copy-done.2
  9.8 1.9 %copy.24 = f32[1,1,548,1024]{3,2,1,0:T(8,128)} copy(f32[1,1,548,1024]{3,1,2,0:T(1,128)S(1)} %copy-done.2) | data formatting | bytes 4489216
  11.7 4.8 %pack.1.packed_ref = f32[1224,128]{1,0:T(8,128)} custom-call(f32[548,1024]{1,0:T(8,128)} %bitcast.21, f32[1,1024]{1,0:T(1,128)} %bitcast.26, s32[1,1024]{1,0:T(1,128)} %bitcast.27), custom_call_target="tpu_custom_call" | custom-call | tf_op jit(solution)/shard_map/pack/pallas_call | solution.py:79
  16.4 5.6 %copy_bitcast_fusion.1 = (f32[548,1024]{1,0:T(8,128)}, f32[548,1024]{1,0:T(8,128)}) fusion(f32[1,548,1024]{2,0,1:T(1,128)} %param.10, f32[1,548,1024]{2,0,1:T(1,128)} %param.9), kind=kLoop, calls=%fused_computation.1 | loop fusion | bytes 8978432
  22.0 85.1 %sweep.1 = (f32[548,1024]{1,0:T(8,128)}, f32[548,1024]{1,0:T(8,128)}, f32[32,1224,128]{2,1,0:T(8,128)}) custom-call(f32[548,1024]{1,0:T(8,128)} %bitcast.20, f32[548,1024]{1,0:T(8,128)} %get-tuple-element.15.two_ref, f32[548,1024]{1,0:T(8,128)} %get-tuple-element.14.gain_ref, f32[548,548]{1,0:T(8,128)} %bitcast.22, f32[548,548]{1,0:T(8,128)} %bitcast.23, ...), custom_call_target="tpu_custom_call" | custom-call | tf_op jit(solution)/shard_map/sweep/pallas_call | solution.py:331
  107.1 34.3 %apply.1 = (f32[548,1024]{1,0:T(8,128)}, f32[548,1024]{1,0:T(8,128)}) custom-call(s32[1,1024]{1,0:T(1,128)} %owner_ref.1, f32[548,1024]{1,0:T(8,128)} %get-tuple-element.7.forward_ref, f32[548,1024]{1,0:T(8,128)} %get-tuple-element.8.swept_ref, f32[32,1224,128]{2,1,0:T(8,128)} %get-tuple-element.9.gathered_ref), custom_call_target="tpu_custom_call" | custom-call | tf_op jit(solution)/shard_map/apply/pallas_call | solution.py:459
  141.5 0.0 copy-start.1
  141.5 5.5 %copy.12 = f32[1,548,1024]{2,0,1:T(1,128)} copy(f32[1,548,1024]{2,1,0:T(8,128)} %bitcast.25) | data formatting | bytes 4489216
  146.9 0.0 copy-done.1
  146.9 3.7 %copy.13 = f32[1,548,1024]{2,0,1:T(1,128)} copy(f32[1,548,1024]{2,1,0:T(8,128)S(1)} %bitcast.24) | data formatting | bytes 4489216
Async XLA Ops:
  0.6 2.7 %copy-start = (f32[1,548,548]{2,0,1:T(1,128)S(1)}, f32[1,548,548]{2,0,1:T(1,128)}, u32[]{:S(2)}) copy-start(f32[1,548,548]{2,0,1:T(1,128)} %param.11) | copy-start | bytes 3603652
  6.0 3.7 %copy-start.2 = (f32[1,1,548,1024]{3,1,2,0:T(1,128)S(1)}, f32[1,1,548,1024]{3,1,2,0:T(1,128)}, u32[]{:S(2)}) copy-start(f32[1,1,548,1024]{3,1,2,0:T(1,128)} %param.13) | copy-start | bytes 6733828
  141.5 5.5 %copy-start.1 = (f32[548,1024]{1,0:T(8,128)S(1)}, f32[548,1024]{1,0:T(8,128)}, u32[]{:S(2)}) copy-start(f32[548,1024]{1,0:T(8,128)} %get-tuple-element.11) | copy-start | bytes 6733828
where the time goes:
time: 152 us; the launch traced here: 151 us
  Pallas kernels  124 us (82%)
  local copies, waits for them, and re-layouts  25.7 us (17%)
    pallas_call x1, Pallas kernels, sweep(): pl.pallas_call(sweep_kernel, out_shape=(jax.ShapeDtypeStruct((rows, cols)...  85.1 us
    pallas_call x1, Pallas kernels, apply(): pl.pallas_call(apply_kernel, grid=(8,), out_shape=(jax.ShapeDtypeStruct((...  34.3 us
    unnamed x12, local copies, waits for them, and re-layouts  23.1 us
    pallas_call x1, Pallas kernels, pack(): pl.pallas_call(pack_kernel, out_shape=jax.ShapeDtypeStruct((PACKED, 128),...  4.79 us

commit v1 on v0

--- a/solution.py
+++ b/solution.py
@@ -32,9 +32,7 @@
     return lax.dot_general(a, b, (((1,), (1,)), ((), ())), preferred_element_type=F32)
 
 
-def pack_kernel(matrix_ref, error_ref, mask_ref, out_ref):
-    weight = error_ref[...] * mask_ref[...].astype(F32)
-    matrix = matrix_ref[...]
+def form_packed(matrix, weight, out_ref):
     high, low = split(matrix)
     whigh, wlow = split(matrix * weight)
 
@@ -75,19 +73,12 @@
             out_ref[at : at + rest, 0:rest] = tail[:, 512:nv]
 
 
-def pack(jacobian, error, mask):
-    return pl.pallas_call(
-        pack_kernel,
-        out_shape=jax.ShapeDtypeStruct((PACKED, 128), F32),
-        name="pack",
-    )(jacobian, error, mask)
-
-
 def sweep_kernel(
-    one_ref, two_ref, gain_ref, matrix_ref, turned_ref, packed_ref,
-    forward_ref, swept_ref, gathered_ref,
-    into_f, into_b, out_b, m_high, m_low, t_high, t_low,
-    f_send, f_recv, b_send, b_recv, g_send, g_recv, p_send, p_recv, own_sem,
+    one_hbm, two_hbm, gain_hbm, matrix_hbm, jacobian_hbm, error_ref, mask_ref,
+    forward_out, swept_out, gathered_ref,
+    one, two, gain, forward, swept, into_f, into_b, out_b, matrix, jacobian, packed_ref,
+    m_high, m_low, t_high, t_low,
+    load_sem, store_sem, matrix_sem, f_send, f_recv, b_send, b_recv, g_send, g_recv, p_send, p_recv, own_sem,
 ):
     k = lax.axis_index("tm")
     region = lax.axis_index("region")
@@ -100,15 +91,42 @@
         return ((z + dz + 4) % 4 * 4 + (x + dx + 4) % 4) * 2 + core
 
     partner = region + 1 - 2 * core
+
+    def load(which, c):
+        hbm, vmem = ((one_hbm, one), (two_hbm, two), (gain_hbm, gain))[which]
+        return pltpu.make_async_copy(
+            hbm.at[:, 0, pl.ds(c * CHUNK, CHUNK)], vmem.at[c], load_sem.at[which, c]
+        )
+
+    def load_at(which, c):
+        hbm, vmem = ((one_hbm, one), (two_hbm, two), (gain_hbm, gain))[which]
+        return pltpu.make_async_copy(
+            hbm.at[:, 0, pl.ds(pl.multiple_of(c * CHUNK, CHUNK), CHUNK)], vmem.at[c], load_sem.at[which, c]
+        )
+
+    matrix_copy = pltpu.make_async_copy(matrix_hbm.at[:, 0, :], matrix, matrix_sem.at[0])
+    jacobian_copy = pltpu.make_async_copy(jacobian_hbm.at[:, 0, :], jacobian, matrix_sem.at[1])
+    load(0, 0).start()
+    matrix_copy.start()
+    load(1, 0).start()
+    load(2, 0).start()
+    jacobian_copy.start()
+    for c in range(1, chunks):
+        for which in range(3):
+            load(which, c).start()
+
+    def store_f(src, c):
+        return pltpu.make_async_copy(src, forward_out.at[c], store_sem.at[0, c])
+
+    def store_b(src, c):
+        return pltpu.make_async_copy(src, swept_out.at[c], store_sem.at[1, c])
+
     barrier = pltpu.get_barrier_semaphore()
     around = [(k, chip(1, 0)), (k, chip(-1, 0)), (k, chip(0, 1)), (k, chip(0, -1)), (k, partner),
               ((k + 1) % 4, region), ((k + 3) % 4, region)]
     for who in around:
         pl.semaphore_signal(barrier, inc=1, device_id=who, device_id_type=MESH)
     pl.semaphore_wait(barrier, len(around))
-
-    def columns(c):
-        return pl.ds(pl.multiple_of(c * CHUNK, CHUNK), CHUNK)
 
     def send_f(src, c):
         return pltpu.make_async_remote_copy(
@@ -216,28 +234,17 @@
         arrived(half, dp, 2, 1)
         share(half, dp, 2)
 
-    for half in range(2):
-        main, _ = axes[half]
-        relay(half, 0, 0, None, main, 1)
-        relay(half, 0, 0, None, main, -1)
-    for half in range(2):
-        _, other = axes[half]
-        relay(half, 0, 0, None, other, 1)
-        relay(half, 0, 0, None, other, -1)
-
     @pl.when(k == 0)
     def _():
         for c in range(chunks):
-            send_f(one_ref.at[:, c * CHUNK : (c + 1) * CHUNK], c).start()
-
-    for half in range(2):
-        share(half, 0, 0)
-    own_copy = pltpu.make_async_copy(packed_ref, gathered_ref.at[region], own_sem)
-    own_copy.start()
-
-    high, low = split(matrix_ref[...])
+            load(0, c).wait()
+            send_f(one.at[c], c).start()
+            store_f(one.at[c], c).start()
+
+    matrix_copy.wait()
+    high, low = split(matrix[...])
     m_high[...], m_low[...] = high, low
-    high, low = split(turned_ref[...])
+    high, low = split(matrix[...].T)
     t_high[...], t_low[...] = high, low
 
     def times(a_high, a_low, v):
@@ -258,40 +265,70 @@
     }
 
     def tick(t, carry):
+        cf = t - k
+
+        @pl.when((cf >= 0) & (cf < chunks) & (k > 0))
+        def _():
+            load_at(0, cf).wait()
+
+            @pl.when(k == 1)
+            def _():
+                load_at(2, cf).wait()
+
+            send_f(into_f.at[cf], cf).wait_recv()
+            forward[cf] = one[cf] + gain[cf] * times(m_high, m_low, into_f[cf])
+
+            @pl.when(k < 3)
+            def _():
+                send_f(forward.at[cf], cf).start()
+
+            store_f(forward.at[cf], cf).start()
+
         cb = t - (3 - k)
 
         @pl.when((cb >= 0) & (cb < chunks))
         def _():
+            load_at(1, cb).wait()
+
+            @pl.when(k != 1)
+            def _():
+                load_at(2, cb).wait()
+
             @pl.when(k < 3)
             def _():
                 send_b(cb).wait_recv()
-                swept_ref[:, columns(cb)] = two_ref[:, columns(cb)] + into_b[cb]
+                swept[cb] = two[cb] + into_b[cb]
 
             @pl.when(k == 3)
             def _():
-                swept_ref[:, columns(cb)] = two_ref[:, columns(cb)]
+                swept[cb] = two[cb]
 
             @pl.when(k > 0)
             def _():
-                out_b[cb] = times(t_high, t_low, gain_ref[:, columns(cb)] * swept_ref[:, columns(cb)])
+                out_b[cb] = times(t_high, t_low, gain[cb] * swept[cb])
                 send_b(cb).start()
 
-        cf = t - k
-
-        @pl.when((cf >= 0) & (cf < chunks) & (k > 0))
-        def _():
-            send_f(into_f.at[cf], cf).wait_recv()
-            forward_ref[:, columns(cf)] = one_ref[:, columns(cf)] + gain_ref[:, columns(cf)] * times(
-                m_high, m_low, into_f[cf]
-            )
-
-            @pl.when(k < 3)
-            def _():
-                send_f(forward_ref.at[:, columns(cf)], cf).start()
+            store_b(swept.at[cb], cb).start()
 
         return carry
 
-    at = 0
+    lax.fori_loop(0, 1, tick, 0)
+    jacobian_copy.wait()
+    form_packed(jacobian[...], error_ref[...] * mask_ref[...].astype(F32), packed_ref)
+    for half in range(2):
+        main, _ = axes[half]
+        relay(half, 0, 0, None, main, 1)
+        relay(half, 0, 0, None, main, -1)
+    for half in range(2):
+        _, other = axes[half]
+        relay(half, 0, 0, None, other, 1)
+        relay(half, 0, 0, None, other, -1)
+    for half in range(2):
+        share(half, 0, 0)
+    own_copy = pltpu.make_async_copy(packed_ref, gathered_ref.at[region], own_sem)
+    own_copy.start()
+
+    at = 1
     for tick_end in sorted(events):
         lax.fori_loop(at, tick_end + 1, tick, 0)
         at = tick_end + 1
@@ -299,9 +336,9 @@
             event[0](*event[1:])
     lax.fori_loop(at, chunks + 3, tick, 0)
 
-    @pl.when(k == 0)
-    def _():
-        forward_ref[...] = one_ref[...]
+    for c in range(chunks):
+        store_f(forward.at[c], c).wait()
+        store_b(swept.at[c], c).wait()
 
     @pl.when(k < 3)
     def _():
@@ -324,27 +361,29 @@
         pltpu.make_async_copy(ref, ref, p_recv.at[half, dp % 4 * 4 + dq % 4]).wait()
 
 
-def sweep(one, two, gain, matrix, turned, packed):
-    rows, cols = one.shape
+def sweep(one, two, gain, matrix, jacobian, error, mask):
+    rows, _, cols = one.shape
     chunks = cols // CHUNK
     vmem = pl.BlockSpec(memory_space=pltpu.VMEM)
+    hbm = pl.BlockSpec(memory_space=pl.ANY)
+    chunked = (chunks, rows, CHUNK)
+    square = (rows, rows)
     return pl.pallas_call(
         sweep_kernel,
         out_shape=(
-            jax.ShapeDtypeStruct((rows, cols), F32),
-            jax.ShapeDtypeStruct((rows, cols), F32),
+            jax.ShapeDtypeStruct(chunked, F32),
+            jax.ShapeDtypeStruct(chunked, F32),
             jax.ShapeDtypeStruct((32, PACKED, 128), F32),
         ),
-        in_specs=[vmem] * 6,
-        out_specs=(vmem, vmem, pl.BlockSpec(memory_space=pl.ANY)),
-        scratch_shapes=[
-            pltpu.VMEM((chunks, rows, CHUNK), F32),
-            pltpu.VMEM((chunks, rows, CHUNK), F32),
-            pltpu.VMEM((chunks, rows, CHUNK), F32),
-            pltpu.VMEM((rows, rows), BF16),
-            pltpu.VMEM((rows, rows), BF16),
-            pltpu.VMEM((rows, rows), BF16),
-            pltpu.VMEM((rows, rows), BF16),
+        in_specs=[hbm] * 5 + [vmem] * 2,
+        out_specs=(hbm, hbm, hbm),
+        scratch_shapes=[pltpu.VMEM(chunked, F32)] * 8
+        + [pltpu.VMEM(square, F32), pltpu.VMEM((rows, cols), F32), pltpu.VMEM((PACKED, 128), F32)]
+        + [pltpu.VMEM(square, BF16)] * 4
+        + [
+            pltpu.SemaphoreType.DMA((3, chunks)),
+            pltpu.SemaphoreType.DMA((2, chunks)),
+            pltpu.SemaphoreType.DMA((2,)),
             pltpu.SemaphoreType.DMA((chunks,)),
             pltpu.SemaphoreType.DMA((chunks,)),
             pltpu.SemaphoreType.DMA((chunks,)),
@@ -359,16 +398,17 @@
             collective_id=0, has_side_effects=True, vmem_limit_bytes=60 * 1024 * 1024
         ),
         name="sweep",
-    )(one, two, gain, matrix, turned, packed)
+    )(one, two, gain, matrix, jacobian, error, mask)
 
 
 def apply_kernel(
     owner_ref, forward_ref, swept_ref, gathered_ref,
     state_ref, gradient_ref,
-    x_high, x_low, slot_row, slot_col, full, right,
+    x_high, x_low, slot_row, slot_col, full, right, total,
 ):
     step = pl.program_id(0)
-    rows, cols = forward_ref.shape
+    rows, cols = total.shape
+    chunks = cols // CHUNK
     pad = full.shape[1] // 2
 
     @pl.when(step == 0)
@@ -383,10 +423,13 @@
         slot = owner.astype(F32) * SLOT + placed
         slot_row[...] = jnp.broadcast_to(slot, slot_row.shape)
         slot_col[...] = jnp.broadcast_to(slot, (128, cols)).T
-        high, low = split(forward_ref[...])
-        x_high[...], x_low[...] = high, low
-        state_ref[...] = forward_ref[...]
-        gradient_ref[...] = swept_ref[...]
+        for c in range(chunks):
+            value = forward_ref[c]
+            high, low = split(value)
+            lanes = slice(c * CHUNK, (c + 1) * CHUNK)
+            x_high[:, lanes], x_low[:, lanes] = high, low
+            state_ref[:, c, :] = value
+            total[:, lanes] = swept_ref[c]
         right[...] = jnp.zeros_like(right)
         full[...] = jnp.zeros_like(full)
 
@@ -449,24 +492,31 @@
             jnp.where(left_lanes, even + pltpu.roll(even, SLOT, 1), odd + pltpu.roll(odd, SLOT, 1))
         )
     high, low = split(jnp.concatenate(answers, axis=1))
-    gradient_ref[...] += dot(high, place) + dot(low, place)
+    total[...] += dot(high, place) + dot(low, place)
+
+    @pl.when(step == pl.num_programs(0) - 1)
+    def _():
+        for c in range(chunks):
+            gradient_ref[:, c, :] = total[:, c * CHUNK : (c + 1) * CHUNK]
 
 
 def apply(owner, forward, swept, gathered):
-    rows, cols = forward.shape
-    whole = pl.BlockSpec((rows, cols), lambda i: (0, 0))
+    chunks, rows, _ = forward.shape
+    cols = chunks * CHUNK
+    whole = pl.BlockSpec((chunks, rows, CHUNK), lambda i: (0, 0, 0))
+    result = pl.BlockSpec((rows, chunks, CHUNK), lambda i: (0, 0, 0))
     pad = 640
     return pl.pallas_call(
         apply_kernel,
         grid=(8,),
-        out_shape=(jax.ShapeDtypeStruct((rows, cols), F32), jax.ShapeDtypeStruct((rows, cols), F32)),
+        out_shape=(jax.ShapeDtypeStruct((rows, chunks, CHUNK), F32),) * 2,
         in_specs=[
             pl.BlockSpec((1, cols), lambda i: (0, 0)),
             whole,
             whole,
             pl.BlockSpec((4, PACKED, 128), lambda i: (i, 0, 0)),
         ],
-        out_specs=(whole, whole),
+        out_specs=(result, result),
         scratch_shapes=[
             pltpu.VMEM((rows, cols), BF16),
             pltpu.VMEM((rows, cols), BF16),
@@ -474,19 +524,25 @@
             pltpu.VMEM((cols, 128), F32),
             pltpu.VMEM((rows, 2 * pad), BF16),
             pltpu.VMEM((2 * pad, 128), BF16),
+            pltpu.VMEM((rows, cols), F32),
         ],
         compiler_params=pltpu.CompilerParams(vmem_limit_bytes=60 * 1024 * 1024),
         name="apply",
     )(owner, forward, swept, gathered)
 
 
+def by_row(x):
+    return jnp.transpose(x, (1, 0, 2))
+
+
 def body(search_one, search_two, column_gain, model_matrix, obs_owner, observe_matrix, error_weight, channel_mask):
-    packed = pack(observe_matrix[0, 0], error_weight[0], channel_mask[0])
+    rows, cols = search_one.shape[1:]
     forward, swept, gathered = sweep(
-        search_one[0], search_two[0], column_gain[0], model_matrix[0], model_matrix[0].T, packed
+        by_row(search_one), by_row(search_two), by_row(column_gain), by_row(model_matrix),
+        by_row(observe_matrix[0]), error_weight[0], channel_mask[0],
     )
     state, gradient = apply(obs_owner, forward, swept, gathered)
-    return state[None], gradient[None]
+    return tuple(by_row(out.reshape(rows, 1, cols)) for out in (state, gradient))
 
 
 def solution(mesh):

time: 152 us -> 123 us (0.81)
  local copies, waits for them, and re-layouts: 25.7 us -> 0 us
  Pallas kernels: 124 us -> 122 us
    unnamed x12 -> x0, local copies, waits for them, and re-layouts: 23.1 us -> none
    pallas_call x2 -> x1, Pallas kernels: 89.9 us -> 84.3 us  [sweep(): pl.pallas_call(sweep_kernel, out_shape=(jax.ShapeDtypeStruct(chunked, F32...]
    pallas_call x1, Pallas kernels: 34.3 us -> 37.7 us  [apply(): pl.pallas_call(apply_kernel, grid=(8,), out_shape=(jax.ShapeDtypeStruct((...]
    squeeze x1 -> x0, local copies, waits for them, and re-layouts: 2.64 us -> none  [body(): model_matrix[0]]
where the time goes in v1:
time: 123 us
  Pallas kernels  122 us (99%)
    pallas_call x1, Pallas kernels, sweep(): pl.pallas_call(sweep_kernel, out_shape=(jax.ShapeDtypeStruct(chunked, F32...  84.3 us
    pallas_call x1, Pallas kernels, apply(): pl.pallas_call(apply_kernel, grid=(8,), out_shape=(jax.ShapeDtypeStruct((...  37.7 us

profile of v1, /device:TPU:1, one launch (start us, length us, event | category | flops | bytes accessed | tf_op | source)
XLA Modules:
  0.0 122.7 jit_solution(997153028629123251)
XLA Ops:
  0.6 84.3 %sweep.1 = (f32[8,548,128]{2,1,0:T(8,128)}, f32[8,548,128]{2,1,0:T(8,128)}, f32[32,1224,128]{2,1,0:T(8,128)}) custom-call(f32[548,1,1024]{2,1,0:T(1,128)} %bitcast.9, f32[548,1,1024]{2,1,0:T(1,128)} %bitcast.10, f32[548,1,1024]{2,1,0:T(1,128)} %bitcast.11, f32[548,1,548]{2,1,0:T(1,128)} %bitcast.13, f32[548,1,1024]{2,1,0:T(1,128)} %bitcast.12, ...), custom_call_target="tpu_custom_call" | custom-call | tf_op jit(solution)/shard_map/sweep/pallas_call | solution.py:371
  84.9 37.7 %apply.1 = (f32[548,8,128]{2,1,0:T(8,128)}, f32[548,8,128]{2,1,0:T(8,128)}) custom-call(s32[1,1024]{1,0:T(1,128)} %owner_ref.1, f32[8,548,128]{2,1,0:T(8,128)} %get-tuple-element.7.forward_ref, f32[8,548,128]{2,1,0:T(8,128)} %get-tuple-element.8.swept_ref, f32[32,1224,128]{2,1,0:T(8,128)} %get-tuple-element.9.gathered_ref), custom_call_target="tpu_custom_call" | custom-call | tf_op jit(solution)/shard_map/apply/pallas_call | solution.py:509

commit v2 on v1

v2 whole, which is shorter than its diff:
```python
import jax
import jax.numpy as jnp
from jax import lax
from jax.experimental import pallas as pl
from jax.experimental.pallas import tpu as pltpu
from jax.sharding import PartitionSpec as P

F32 = jnp.float32
BF16 = jnp.bfloat16
MESH = pl.DeviceIdType.MESH

OFFDIAG = ((0, 1), (0, 2), (0, 3), (1, 2), (1, 3), (2, 3))
FOLD_AT = 768
TAIL_AT = 1024
TAIL = 40
PACKED = TAIL_AT + 5 * TAIL
HALVES = ((0, 616, 312), (616, 608, 304))
SLOT = 64
CHUNK = 128
FOLDED = 276


def split(x):
    high = x.astype(BF16)
    return high, (x - high.astype(F32)).astype(BF16)


def dot(a, b):
    return jnp.dot(a, b, preferred_element_type=F32)


def dot_nt(a, b):
    return lax.dot_general(a, b, (((1,), (1,)), ((), ())), preferred_element_type=F32)


def form_packed(matrix, weight, out_ref):
    high, low = split(matrix)
    whigh, wlow = split(matrix * weight)

    def product(r0, r1, c0, c1):
        a, b = slice(r0, r1), slice(c0, c1)
        return dot_nt(whigh[a], high[b]) + (dot_nt(whigh[a], low[b]) + dot_nt(wlow[a], high[b]))

    top = product(0, 256, 0, 512)
    mid = product(256, 512, 256, 512)
    nv = matrix.shape[0]
    tail = product(512, nv, 0, nv)

    def block(i, j):
        if i < 2:
            return top[128 * i : 128 * i + 128, 128 * j : 128 * j + 128]
        return mid[128 * i - 256 : 128 * i - 128, 128 * j - 256 : 128 * j - 128]

    for at, (i, j) in enumerate(OFFDIAG):
        out_ref[128 * at : 128 * at + 128, :] = block(i, j)
    row = lax.broadcasted_iota(jnp.int32, (128, 128), 0)
    col = lax.broadcasted_iota(jnp.int32, (128, 128), 1)
    for pair in range(2):
        upper, lower = block(2 * pair, 2 * pair), block(2 * pair + 1, 2 * pair + 1)
        at = FOLD_AT + 128 * pair
        out_ref[at : at + 128, :] = jnp.where(row <= col, upper, lower)
    rest = nv - 512
    for j in range(5):
        at = TAIL_AT + TAIL * j
        if j < 4:
            out_ref[at : at + rest, :] = tail[:, 128 * j : 128 * j + 128]
            if j % 2 == 1:
                line = jnp.sum(jnp.where(row == col, block(j, j), 0.0), axis=0, keepdims=True)
            else:
                line = jnp.zeros((1, 128), F32)
            out_ref[at + rest : at + TAIL, :] = jnp.broadcast_to(line, (TAIL - rest, 128))
        else:
            out_ref[at : at + TAIL, :] = jnp.zeros((TAIL, 128), F32)
            out_ref[at : at + rest, 0:rest] = tail[:, 512:nv]


def sweep_kernel(
    one_hbm, two_hbm, gain_hbm, matrix_hbm, jacobian_hbm, error_ref, mask_ref,
    forward_out, swept_out, gathered_ref,
    one, two, gain, forward, swept, into_f, into_b, out_f, out_b, matrix, jacobian, packed_ref,
    m_high, m_low, t_high, t_low,
    load_sem, store_sem, matrix_sem, f_send, f_recv, b_send, b_recv, g_send, g_recv, p_send, p_recv, own_sem,
):
    k = lax.axis_index("tm")
    region = lax.axis_index("region")
    core = region % 2
    x = (region // 2) % 4
    z = region // 8
    chunks, rows, _ = one.shape
    pieces = 2 * chunks
    cut = rows - FOLDED

    def chip(dz, dx):
        return ((z + dz + 4) % 4 * 4 + (x + dx + 4) % 4) * 2 + core

    partner = region + 1 - 2 * core

    def load(which, c):
        hbm, vmem = ((one_hbm, one), (two_hbm, two), (gain_hbm, gain))[which]
        return pltpu.make_async_copy(
            hbm.at[:, 0, pl.ds(c * CHUNK, CHUNK)], vmem.at[c], load_sem.at[which, c]
        )

    def load_at(which, c):
        hbm, vmem = ((one_hbm, one), (two_hbm, two), (gain_hbm, gain))[which]
        return pltpu.make_async_copy(
            hbm.at[:, 0, pl.ds(pl.multiple_of(c * CHUNK, CHUNK), CHUNK)], vmem.at[c], load_sem.at[which, c]
        )

    matrix_copy = pltpu.make_async_copy(matrix_hbm.at[:, 0, :], matrix, matrix_sem.at[0])
    jacobian_copy = pltpu.make_async_copy(jacobian_hbm.at[:, 0, :], jacobian, matrix_sem.at[1])
    load(0, 0).start()
    matrix_copy.start()
    load(1, 0).start()
    load(2, 0).start()
    jacobian_copy.start()
    for c in range(1, chunks):
        for which in range(3):
            load(which, c).start()

    def store_f(src, c):
        return pltpu.make_async_copy(src, forward_out.at[c], store_sem.at[0, c])

    def store_b(src, c):
        return pltpu.make_async_copy(src, swept_out.at[c], store_sem.at[1, c])

    barrier = pltpu.get_barrier_semaphore()
    around = [(k, chip(1, 0)), (k, chip(-1, 0)), (k, chip(0, 1)), (k, chip(0, -1)), (k, partner),
              ((k + 1) % 4, region), ((k + 3) % 4, region)]
    for who in around:
        pl.semaphore_signal(barrier, inc=1, device_id=who, device_id_type=MESH)
    pl.semaphore_wait(barrier, len(around))

    def send_f(s):
        return pltpu.make_async_remote_copy(
            src_ref=out_f.at[s], dst_ref=into_f.at[s], send_sem=f_send.at[s], recv_sem=f_recv.at[s],
            device_id=((k + 1) % 4, region), device_id_type=MESH,
        )

    def send_b(s):
        return pltpu.make_async_remote_copy(
            src_ref=out_b.at[s], dst_ref=into_b.at[s], send_sem=b_send.at[s], recv_sem=b_recv.at[s],
            device_id=((k + 3) % 4, region), device_id_type=MESH,
        )

    def step_to(primary, by):
        return chip(by, 0) if primary == "z" else chip(0, by)

    def block_at(half, dp, dq):
        if half == 0:
            return chip(dq, dp)
        return chip(dp, dq)

    axes = (("x", "z"), ("z", "x"))
    sends = []

    def span(half, piece):
        start, size, first_part = HALVES[half]
        if piece == 0:
            return start, first_part
        if piece == 1:
            return start + first_part, size - first_part
        return start, size

    def relay_copy(number, half, dp, dq, piece, axis, by):
        start, size = span(half, piece)
        block = block_at(half, dp, dq)
        own = dp == 0 and dq == 0
        place = pl.ds(start, size)
        rp, rq = dp % 4, dq % 4
        if axis == axes[half][0]:
            rp = (dp - by) % 4
        else:
            rq = (dq - by) % 4
        return pltpu.make_async_remote_copy(
            src_ref=packed_ref.at[place] if own else gathered_ref.at[block, place],
            dst_ref=gathered_ref.at[block, place],
            send_sem=g_send.at[number],
            recv_sem=g_recv.at[half, rp * 4 + rq, 1 if piece == 1 else 0],
            device_id=(k, step_to(axis, by)),
            device_id_type=MESH,
        )

    def relay(*what):
        relay_copy(len(sends), *what).start()
        sends.append(what)

    def arrived(half, dp, dq, piece):
        start, size = span(half, piece)
        block = block_at(half, dp, dq)
        ref = gathered_ref.at[block, pl.ds(start, size)]
        sem = g_recv.at[half, dp % 4 * 4 + dq % 4, 1 if piece == 1 else 0]
        pltpu.make_async_copy(ref, ref, sem).wait()

    shared = []

    def share_copy(half, dp, dq):
        start, size = span(half, None)
        block = block_at(half, dp, dq)
        place = pl.ds(start, size)
        own = dp == 0 and dq == 0
        at = dp % 4 * 4 + dq % 4
        return pltpu.make_async_remote_copy(
            src_ref=packed_ref.at[place] if own else gathered_ref.at[block, place],
            dst_ref=gathered_ref.at[block, place],
            send_sem=p_send.at[half, at],
            recv_sem=p_recv.at[half, at],
            device_id=(k, partner),
            device_id_type=MESH,
        )

    def share(*what):
        share_copy(*what).start()
        shared.append(what)

    def first(half, by):
        main, other = axes[half]
        arrived(half, by, 0, None)
        relay(half, by, 0, 0 if by == -1 else 1, main, -by)
        relay(half, by, 0, None, other, 1)
        relay(half, by, 0, None, other, -1)
        share(half, by, 0)

    def opposite(half):
        _, other = axes[half]
        arrived(half, 2, 0, 0)
        arrived(half, 2, 0, 1)
        relay(half, 2, 0, None, other, 1)
        relay(half, 2, 0, None, other, -1)
        share(half, 2, 0)

    def second(half, dp, by):
        _, other = axes[half]
        arrived(half, dp, by, None)
        relay(half, dp, by, 0 if by == -1 else 1, other, -by)
        share(half, dp, by)

    def last(half, dp):
        arrived(half, dp, 2, 0)
        arrived(half, dp, 2, 1)
        share(half, dp, 2)

    left = lax.broadcasted_iota(jnp.int32, (FOLDED, CHUNK), 1) < CHUNK // 2

    def fold(v, h):
        top = pltpu.roll(v[0:FOLDED], CHUNK // 2 * h, 1)
        low = pltpu.roll(v[cut:rows], CHUNK // 2 * (1 - h), 1)
        return jnp.where(left, top, low)

    def unfold(target, c, one_half, other_half, add):
        turned, returned = pltpu.roll(one_half, CHUNK // 2, 1), pltpu.roll(other_half, CHUNK // 2, 1)
        top, low = jnp.where(left, one_half, returned), jnp.where(left, turned, other_half)
        if add is not None:
            top, low = add[0:FOLDED] + top, add[cut:rows] + low
        target[c, 0:FOLDED, :] = top
        target[c, cut:rows, :] = low

    def times(a_high, a_low, v):
        high = v.astype(BF16).astype(F32)
        low = pltpu.roll(v - high, CHUNK // 2, 1)
        both = jnp.concatenate(
            [jnp.where(left, high, low)[0:cut].astype(BF16), jnp.where(left, low, high).astype(BF16)], axis=0
        )
        alone = jnp.concatenate(
            [jnp.where(left, high, 0.0)[0:cut].astype(BF16), jnp.where(left, 0.0, high).astype(BF16)], axis=0
        )
        total = dot(a_high[...], both) + dot(a_low[...], alone)
        total = total + pltpu.roll(total, CHUNK // 2, 1)
        return jnp.where(left, total[0:FOLDED], total[cut:rows])

    def leave(c):
        load_at(0, c).wait()
        value = one[c]
        for h in range(2):
            out_f[2 * c + h] = fold(value, h)
            send_f(2 * c + h).start()
        store_f(one.at[c], c).start()

    def prepare():
        matrix_copy.wait()
        value = matrix[...]
        m_high[...], m_low[...] = split(value)
        t_high[...], t_low[...] = split(value.T)

    def forward_step(s):
        c, h = s // 2, s % 2

        @pl.when(h == 0)
        def _():
            load_at(0, c).wait()

            @pl.when(k == 1)
            def _():
                load_at(2, c).wait()

        send_f(s).wait_recv()
        out_f[s] = fold(one[c], h) + fold(gain[c], h) * times(m_high, m_low, into_f[s])

        @pl.when(k < 3)
        def _():
            send_f(s).start()

        @pl.when(h == 1)
        def _():
            unfold(forward, c, out_f[s - 1], out_f[s], None)
            store_f(forward.at[c], c).start()

    def backward_step(s):
        c, h = s // 2, s % 2

        @pl.when(h == 0)
        def _():
            load_at(1, c).wait()

            @pl.when(k != 1)
            def _():
                load_at(2, c).wait()

        @pl.when(k < 3)
        def _():
            send_b(s).wait_recv()

        @pl.when(k == 3)
        def _():
            into_b[s] = jnp.zeros((FOLDED, CHUNK), F32)

        @pl.when(k > 0)
        def _():
            out_b[s] = times(t_high, t_low, fold(gain[c], h) * (fold(two[c], h) + into_b[s]))
            send_b(s).start()

        @pl.when(h == 1)
        def _():
            unfold(swept, c, into_b[s - 1], into_b[s], two[c])
            store_b(swept.at[c], c).start()

    @pl.when(k == 0)
    def _():
        leave(0)
        leave(1)

    @pl.when(k == 3)
    def _():
        prepare()
        backward_step(0)

    jacobian_copy.wait()
    form_packed(jacobian[...], error_ref[...] * mask_ref[...].astype(F32), packed_ref)
    for half in range(2):
        main, _ = axes[half]
        relay(half, 0, 0, None, main, 1)
        relay(half, 0, 0, None, main, -1)
    for half in range(2):
        _, other = axes[half]
        relay(half, 0, 0, None, other, 1)
        relay(half, 0, 0, None, other, -1)
    for half in range(2):
        share(half, 0, 0)
    own_copy = pltpu.make_async_copy(packed_ref, gathered_ref.at[region], own_sem)
    own_copy.start()

    @pl.when(k != 3)
    def _():
        prepare()

    events = {
        2: [(first, 0, -1), (first, 1, -1), (first, 0, 1), (first, 1, 1)],
        4: [(second, 0, 0, -1), (second, 1, 0, -1), (second, 0, 0, 1), (second, 1, 0, 1)],
        5: [(opposite, 0), (opposite, 1)],
        7: [(second, 0, -1, -1), (second, 1, -1, -1), (second, 0, -1, 1), (second, 1, -1, 1)],
        9: [(second, 0, 1, -1), (second, 1, 1, -1), (second, 0, 1, 1), (second, 1, 1, 1)],
        11: [(last, 0, 0), (last, 1, 0)],
        13: [(second, 0, 2, -1), (second, 1, 2, -1), (second, 0, 2, 1), (second, 1, 2, 1)],
        15: [(last, 0, -1), (last, 1, -1), (last, 0, 1), (last, 1, 1)],
        18: [(last, 0, 2), (last, 1, 2)],
    }

    def tick(t, carry):
        @pl.when((k == 0) & (t >= 1) & (t < chunks - 1))
        def _():
            leave(t + 1)

        cf = t - k

        @pl.when((cf >= 0) & (cf < pieces) & (k > 0))
        def _():
            forward_step(cf)

        cb = t - (3 - k)

        @pl.when((cb >= jnp.where(k == 3, 1, 0)) & (cb < pieces))
        def _():
            backward_step(cb)

        for when, what in events.items():

            @pl.when(t == when)
            def _():
                for event in what:
                    event[0](*event[1:])

        return carry

    lax.fori_loop(0, pieces + 3, tick, 0)

    for c in range(chunks):
        store_f(forward.at[c], c).wait()
        store_b(swept.at[c], c).wait()

    @pl.when(k < 3)
    def _():
        for s in range(pieces):
            send_f(s).wait_send()

    @pl.when(k > 0)
    def _():
        for s in range(pieces):
            send_b(s).wait_send()

    own_copy.wait()
    for number, what in enumerate(sends):
        relay_copy(number, *what).wait_send()
    for what in shared:
        share_copy(*what).wait_send()
        half, dp, dq = what
        start, size = span(half, None)
        block = block_at(half, dp, dq) + 1 - 2 * core
        ref = gathered_ref.at[block, pl.ds(start, size)]
        pltpu.make_async_copy(ref, ref, p_recv.at[half, dp % 4 * 4 + dq % 4]).wait()


def sweep(one, two, gain, matrix, jacobian, error, mask):
    rows, _, cols = one.shape
    chunks = cols // CHUNK
    vmem = pl.BlockSpec(memory_space=pltpu.VMEM)
    hbm = pl.BlockSpec(memory_space=pl.ANY)
    chunked = (chunks, rows, CHUNK)
    square = (rows, rows)
    return pl.pallas_call(
        sweep_kernel,
        out_shape=(
            jax.ShapeDtypeStruct(chunked, F32),
            jax.ShapeDtypeStruct(chunked, F32),
            jax.ShapeDtypeStruct((32, PACKED, 128), F32),
        ),
        in_specs=[hbm] * 5 + [vmem] * 2,
        out_specs=(hbm, hbm, hbm),
        scratch_shapes=[pltpu.VMEM(chunked, F32)] * 5
        + [pltpu.VMEM((2 * chunks, FOLDED, CHUNK), F32)] * 4
        + [pltpu.VMEM(square, F32), pltpu.VMEM((rows, cols), F32), pltpu.VMEM((PACKED, 128), F32)]
        + [pltpu.VMEM(square, BF16)] * 4
        + [
            pltpu.SemaphoreType.DMA((3, chunks)),
            pltpu.SemaphoreType.DMA((2, chunks)),
            pltpu.SemaphoreType.DMA((2,)),
            pltpu.SemaphoreType.DMA((2 * chunks,)),
            pltpu.SemaphoreType.DMA((2 * chunks,)),
            pltpu.SemaphoreType.DMA((2 * chunks,)),
            pltpu.SemaphoreType.DMA((2 * chunks,)),
            pltpu.SemaphoreType.DMA((40,)),
            pltpu.SemaphoreType.DMA((2, 16, 2)),
            pltpu.SemaphoreType.DMA((2, 16)),
            pltpu.SemaphoreType.DMA((2, 16)),
            pltpu.SemaphoreType.DMA,
        ],
        compiler_params=pltpu.CompilerParams(
            collective_id=0, has_side_effects=True, vmem_limit_bytes=60 * 1024 * 1024
        ),
        name="sweep",
    )(one, two, gain, matrix, jacobian, error, mask)


def apply_kernel(
    owner_ref, forward_hbm, swept_hbm, gathered_hbm,
    state_hbm, gradient_hbm,
    forward, swept, packed, x_high, x_low, slot_col, place, full, right, y_high, y_low,
    in_sem, packed_sem, out_sem,
):
    chunks, rows, _ = forward.shape
    groups, wide, cols = place.shape
    pad = full.shape[2] // 2
    depth = packed.shape[0]
    each = wide // SLOT
    load_f = [pltpu.make_async_copy(forward_hbm.at[c], forward.at[c], in_sem.at[0, c]) for c in range(chunks)]
    load_s = [pltpu.make_async_copy(swept_hbm.at[c], swept.at[c], in_sem.at[1, c]) for c in range(chunks)]

    def load_g(group, at):
        return pltpu.make_async_copy(
            gathered_hbm.at[pl.ds(group * each, each)], packed.at[at], packed_sem.at[at]
        )

    def store(source, target, which, c):
        return pltpu.make_async_copy(
            source.at[c], target.at[:, 0, pl.ds(c * CHUNK, CHUNK)], out_sem.at[which, c]
        )

    for copy in load_f:
        copy.start()
    for at in range(depth):
        load_g(at, at).start()
    for copy in load_s:
        copy.start()

    owner = owner_ref[...]
    onehot = (owner == lax.broadcasted_iota(jnp.int32, (32, cols), 0)).astype(F32)
    earlier = (
        lax.broadcasted_iota(jnp.int32, (cols, cols), 0) < lax.broadcasted_iota(jnp.int32, (cols, cols), 1)
    ).astype(BF16)
    before = dot(onehot.astype(BF16), earlier)
    placed = jnp.sum(before * onehot, axis=0, keepdims=True)
    slot = owner.astype(F32) * SLOT + placed
    slot_col[...] = jnp.broadcast_to(slot, (128, cols)).T
    line = lax.broadcasted_iota(jnp.int32, (wide, cols), 0).astype(F32)
    for group in range(groups):
        place[group] = (jnp.broadcast_to(slot - group * wide, (wide, cols)) == line).astype(BF16)
    right[...] = jnp.zeros_like(right)
    full[...] = jnp.zeros_like(full)

    for c in range(chunks):
        load_f[c].wait()
        lanes = slice(c * CHUNK, (c + 1) * CHUNK)
        x_high[:, lanes], x_low[:, lanes] = split(forward[c])
        store(forward, state_hbm, 0, c).start()

    row = lax.broadcasted_iota(jnp.int32, (128, 128), 0)
    col = lax.broadcasted_iota(jnp.int32, (128, 128), 1)
    left_lanes = lax.broadcasted_iota(jnp.int32, (rows, 128), 1) < SLOT
    rest = rows - 512

    def put(full, at_row, at_col, value):
        high, low = split(value)
        r, c = value.shape
        full[at_row : at_row + r, at_col : at_col + c] = high
        full[at_row : at_row + r, pad + at_col : pad + at_col + c] = low

    def unpack(g, full):
        for at, (i, j) in enumerate(OFFDIAG):
            value = g[128 * at : 128 * at + 128, :]
            put(full, 128 * i, 128 * j, value)
            put(full, 128 * j, 128 * i, value.T)
        for fold in range(2):
            at = FOLD_AT + 128 * fold
            value = g[at : at + 128, :]
            turned = value.T
            put(full, 256 * fold, 256 * fold, jnp.where(row <= col, value, turned))
            line_at = TAIL_AT + TAIL * (2 * fold + 1) + rest
            diagonal = jnp.broadcast_to(g[line_at : line_at + 1, :], (128, 128))
            lower = jnp.where(row > col, value, jnp.where(row < col, turned, diagonal))
            put(full, 256 * fold + 128, 256 * fold + 128, lower)
        for j in range(5):
            at = TAIL_AT + TAIL * j
            value = g[at : at + rest, :]
            put(full, 512, 128 * j, value)
            if j < 4:
                tall = jnp.concatenate([value, jnp.zeros((128 - rest, 128), F32)], axis=0)
                put(full, 128 * j, 512, tall.T)

    def one_group(group, carry):
        at = lax.rem(group, depth)
        base = (group * wide).astype(F32)
        lane = lax.broadcasted_iota(jnp.int32, (cols, 128), 1).astype(F32) + base
        pick = jnp.concatenate(
            [(slot_col[...] == lane).astype(BF16), (slot_col[...] == lane + 128.0).astype(BF16)], axis=1
        )
        s_high = dot(x_high[...], pick)
        s_low = dot(x_low[...], pick)
        load_g(group, at).wait()
        for pair in range(each // 2):
            lanes = slice(128 * pair, 128 * pair + 128)
            high = s_high[:, lanes]
            low = pltpu.roll(s_low[:, lanes], SLOT, 1)
            outs = []
            for side in range(2):
                mine = left_lanes if side == 0 else jnp.logical_not(left_lanes)
                right[side, 0:rows, :] = jnp.where(mine, high, low).astype(BF16)
                right[side, pad : pad + rows, :] = jnp.where(mine, high, 0.0).astype(BF16)
                unpack(packed.at[at, 2 * pair + side], full.at[side])
                outs.append(dot(full[side], right[side]))
            even, odd = outs
            answer = jnp.where(left_lanes, even + pltpu.roll(even, SLOT, 1), odd + pltpu.roll(odd, SLOT, 1))
            y_high[group, :, lanes], y_low[group, :, lanes] = split(answer)

        @pl.when(group + depth < groups)
        def _():
            load_g(group + depth, at).start()

        return carry

    lax.fori_loop(0, groups, one_group, 0)

    for c in range(chunks):
        load_s[c].wait()
    for tile in range(cols // 256):
        value = None
        lanes = slice(256 * tile, 256 * tile + 256)
        for group in range(groups):
            part = dot(y_high[group], place[group, :, lanes]) + dot(y_low[group], place[group, :, lanes])
            value = part if value is None else value + part
        for c in (2 * tile, 2 * tile + 1):
            swept[c] = swept[c] + value[:, (c % 2) * CHUNK : (c % 2 + 1) * CHUNK]
            store(swept, gradient_hbm, 1, c).start()
    for c in range(chunks):
        store(forward, state_hbm, 0, c).wait()
        store(swept, gradient_hbm, 1, c).wait()


def apply(owner, forward, swept, gathered):
    chunks, rows, _ = forward.shape
    cols = chunks * CHUNK
    hbm = pl.BlockSpec(memory_space=pl.ANY)
    pad = 640
    groups, wide, depth = 8, 4 * SLOT, 3
    return pl.pallas_call(
        apply_kernel,
        out_shape=(jax.ShapeDtypeStruct((rows, 1, cols), F32),) * 2,
        in_specs=[pl.BlockSpec(memory_space=pltpu.VMEM)] + [hbm] * 3,
        out_specs=(hbm, hbm),
        scratch_shapes=[
            pltpu.VMEM((chunks, rows, CHUNK), F32),
            pltpu.VMEM((chunks, rows, CHUNK), F32),
            pltpu.VMEM((depth, wide // SLOT, PACKED, 128), F32),
            pltpu.VMEM((rows, cols), BF16),
            pltpu.VMEM((rows, cols), BF16),
            pltpu.VMEM((cols, 128), F32),
            pltpu.VMEM((groups, wide, cols), BF16),
            pltpu.VMEM((2, rows, 2 * pad), BF16),
            pltpu.VMEM((2, 2 * pad, 128), BF16),
            pltpu.VMEM((groups, rows, wide), BF16),
            pltpu.VMEM((groups, rows, wide), BF16),
            pltpu.SemaphoreType.DMA((2, chunks)),
            pltpu.SemaphoreType.DMA((depth,)),
            pltpu.SemaphoreType.DMA((2, chunks)),
        ],
        compiler_params=pltpu.CompilerParams(vmem_limit_bytes=60 * 1024 * 1024),
        name="apply",
    )(owner, forward, swept, gathered)


def by_row(x):
    return jnp.transpose(x, (1, 0, 2))


def body(search_one, search_two, column_gain, model_matrix, obs_owner, observe_matrix, error_weight, channel_mask):
    forward, swept, gathered = sweep(
        by_row(search_one), by_row(search_two), by_row(column_gain), by_row(model_matrix),
        by_row(observe_matrix[0]), error_weight[0], channel_mask[0],
    )
    state, gradient = apply(obs_owner, forward, swept, gathered)
    return by_row(state), by_row(gradient)


def solution(mesh):
    return jax.shard_map(
        body,
        mesh=mesh,
        in_specs=(
            P("tm", None, "region"),
            P("tm", None, "region"),
            P("tm", None, "region"),
            P("tm", None, None),
            P("tm", "region"),
            P("tm", "region", None, None),
            P("tm", "region", None),
            P("tm", "region", None),
        ),
        out_specs=(P("tm", None, "region"), P("tm", None, "region")),
        check_vma=False,
    )
```

time: 123 us -> 142 us (1.15)
  Pallas kernels: 122 us -> 141 us
    pallas_call x1, Pallas kernels: 84.3 us -> 107 us  [sweep(): pl.pallas_call(sweep_kernel, out_shape=(jax.ShapeDtypeStruct(chunked, F32...]
    pallas_call x1, Pallas kernels: 37.7 us -> 34.2 us  [apply(): pl.pallas_call(apply_kernel, out_shape=(jax.ShapeDtypeStruct((rows, 1, co...]
where the time goes in v2:
time: 142 us
  Pallas kernels  141 us (99%)
    pallas_call x1, Pallas kernels, sweep(): pl.pallas_call(sweep_kernel, out_shape=(jax.ShapeDtypeStruct(chunked, F32...  107 us
    pallas_call x1, Pallas kernels, apply(): pl.pallas_call(apply_kernel, out_shape=(jax.ShapeDtypeStruct((rows, 1, co...  34.2 us

profile of v2, /device:TPU:1, one launch (start us, length us, event | category | flops | bytes accessed | tf_op | source)
XLA Modules:
  0.0 142.3 jit_solution(17333923738040200623)
XLA Ops:
  0.6 107.3 %sweep.1 = (f32[8,548,128]{2,1,0:T(8,128)}, f32[8,548,128]{2,1,0:T(8,128)}, f32[32,1224,128]{2,1,0:T(8,128)}) custom-call(f32[548,1,1024]{2,1,0:T(1,128)} %bitcast.9, f32[548,1,1024]{2,1,0:T(1,128)} %bitcast.10, f32[548,1,1024]{2,1,0:T(1,128)} %bitcast.11, f32[548,1,548]{2,1,0:T(1,128)} %bitcast.13, f32[548,1,1024]{2,1,0:T(1,128)} %bitcast.12, ...), custom_call_target="tpu_custom_call" | custom-call | tf_op jit(solution)/shard_map/sweep/pallas_call | solution.py:439
  107.9 34.2 %apply.1 = (f32[548,1,1024]{2,1,0:T(1,128)}, f32[548,1,1024]{2,1,0:T(1,128)}) custom-call(s32[1,1024]{1,0:T(1,128)} %owner_ref.1, f32[8,548,128]{2,1,0:T(8,128)} %get-tuple-element.7.forward_hbm, f32[8,548,128]{2,1,0:T(8,128)} %get-tuple-element.8.swept_hbm, f32[32,1224,128]{2,1,0:T(8,128)} %get-tuple-element.9.gathered_hbm), custom_call_target="tpu_custom_call" | custom-call | tf_op jit(solution)/shard_map/apply/pallas_call | solution.py:613

commit v3 on v2

--- a/solution.py
+++ b/solution.py
@@ -18,6 +18,7 @@
 SLOT = 64
 CHUNK = 128
 FOLDED = 276
+LAG = 2
 
 
 def split(x):
@@ -364,15 +365,15 @@
         prepare()
 
     events = {
-        2: [(first, 0, -1), (first, 1, -1), (first, 0, 1), (first, 1, 1)],
-        4: [(second, 0, 0, -1), (second, 1, 0, -1), (second, 0, 0, 1), (second, 1, 0, 1)],
-        5: [(opposite, 0), (opposite, 1)],
-        7: [(second, 0, -1, -1), (second, 1, -1, -1), (second, 0, -1, 1), (second, 1, -1, 1)],
-        9: [(second, 0, 1, -1), (second, 1, 1, -1), (second, 0, 1, 1), (second, 1, 1, 1)],
-        11: [(last, 0, 0), (last, 1, 0)],
-        13: [(second, 0, 2, -1), (second, 1, 2, -1), (second, 0, 2, 1), (second, 1, 2, 1)],
-        15: [(last, 0, -1), (last, 1, -1), (last, 0, 1), (last, 1, 1)],
-        18: [(last, 0, 2), (last, 1, 2)],
+        3: [(first, 0, -1), (first, 1, -1), (first, 0, 1), (first, 1, 1)],
+        6: [(second, 0, 0, -1), (second, 1, 0, -1), (second, 0, 0, 1), (second, 1, 0, 1)],
+        8: [(opposite, 0), (opposite, 1)],
+        10: [(second, 0, -1, -1), (second, 1, -1, -1), (second, 0, -1, 1), (second, 1, -1, 1)],
+        12: [(second, 0, 1, -1), (second, 1, 1, -1), (second, 0, 1, 1), (second, 1, 1, 1)],
+        14: [(last, 0, 0), (last, 1, 0)],
+        16: [(second, 0, 2, -1), (second, 1, 2, -1), (second, 0, 2, 1), (second, 1, 2, 1)],
+        18: [(last, 0, -1), (last, 1, -1), (last, 0, 1), (last, 1, 1)],
+        21: [(last, 0, 2), (last, 1, 2)],
     }
 
     def tick(t, carry):
@@ -380,13 +381,13 @@
         def _():
             leave(t + 1)
 
-        cf = t - k
+        cf = t - LAG * k
 
         @pl.when((cf >= 0) & (cf < pieces) & (k > 0))
         def _():
             forward_step(cf)
 
-        cb = t - (3 - k)
+        cb = t - LAG * (3 - k)
 
         @pl.when((cb >= jnp.where(k == 3, 1, 0)) & (cb < pieces))
         def _():
@@ -401,7 +402,7 @@
 
         return carry
 
-    lax.fori_loop(0, pieces + 3, tick, 0)
+    lax.fori_loop(0, pieces + 3 * LAG, tick, 0)
 
     for c in range(chunks):
         store_f(forward.at[c], c).wait()

time: 142 us -> 118 us (0.83)
  Pallas kernels: 141 us -> 117 us
    pallas_call x1, Pallas kernels: 107 us -> 83.2 us  [sweep(): pl.pallas_call(sweep_kernel, out_shape=(jax.ShapeDtypeStruct(chunked, F32...]
where the time goes in v3:
time: 118 us
  Pallas kernels  117 us (99%)
    pallas_call x1, Pallas kernels, sweep(): pl.pallas_call(sweep_kernel, out_shape=(jax.ShapeDtypeStruct(chunked, F32...  83.2 us
    pallas_call x1, Pallas kernels, apply(): pl.pallas_call(apply_kernel, out_shape=(jax.ShapeDtypeStruct((rows, 1, co...  34.2 us

profile of v3, /device:TPU:1, one launch (start us, length us, event | category | flops | bytes accessed | tf_op | source)
XLA Modules:
  0.0 118.2 jit_solution(13318662240959974274)
XLA Ops:
  0.6 83.2 %sweep.1 = (f32[8,548,128]{2,1,0:T(8,128)}, f32[8,548,128]{2,1,0:T(8,128)}, f32[32,1224,128]{2,1,0:T(8,128)}) custom-call(f32[548,1,1024]{2,1,0:T(1,128)} %bitcast.9, f32[548,1,1024]{2,1,0:T(1,128)} %bitcast.10, f32[548,1,1024]{2,1,0:T(1,128)} %bitcast.11, f32[548,1,548]{2,1,0:T(1,128)} %bitcast.13, f32[548,1,1024]{2,1,0:T(1,128)} %bitcast.12, ...), custom_call_target="tpu_custom_call" | custom-call | tf_op jit(solution)/shard_map/sweep/pallas_call | solution.py:440
  83.9 34.2 %apply.1 = (f32[548,1,1024]{2,1,0:T(1,128)}, f32[548,1,1024]{2,1,0:T(1,128)}) custom-call(s32[1,1024]{1,0:T(1,128)} %owner_ref.1, f32[8,548,128]{2,1,0:T(8,128)} %get-tuple-element.7.forward_hbm, f32[8,548,128]{2,1,0:T(8,128)} %get-tuple-element.8.swept_hbm, f32[32,1224,128]{2,1,0:T(8,128)} %get-tuple-element.9.gathered_hbm), custom_call_target="tpu_custom_call" | custom-call | tf_op jit(solution)/shard_map/apply/pallas_call | solution.py:614

commit v4 on v3

--- a/solution.py
+++ b/solution.py
@@ -34,7 +34,7 @@
     return lax.dot_general(a, b, (((1,), (1,)), ((), ())), preferred_element_type=F32)
 
 
-def form_packed(matrix, weight, out_ref):
+def form_packed(matrix, weight, out_ref, depart):
     high, low = split(matrix)
     whigh, wlow = split(matrix * weight)
 
@@ -42,25 +42,27 @@
         a, b = slice(r0, r1), slice(c0, c1)
         return dot_nt(whigh[a], high[b]) + (dot_nt(whigh[a], low[b]) + dot_nt(wlow[a], high[b]))
 
+    nv = matrix.shape[0]
+    rest = nv - 512
+    row = lax.broadcasted_iota(jnp.int32, (128, 128), 0)
+    col = lax.broadcasted_iota(jnp.int32, (128, 128), 1)
     top = product(0, 256, 0, 512)
-    mid = product(256, 512, 256, 512)
-    nv = matrix.shape[0]
-    tail = product(512, nv, 0, nv)
 
     def block(i, j):
         if i < 2:
             return top[128 * i : 128 * i + 128, 128 * j : 128 * j + 128]
         return mid[128 * i - 256 : 128 * i - 128, 128 * j - 256 : 128 * j - 128]
 
-    for at, (i, j) in enumerate(OFFDIAG):
+    for at, (i, j) in enumerate(OFFDIAG[:5]):
         out_ref[128 * at : 128 * at + 128, :] = block(i, j)
-    row = lax.broadcasted_iota(jnp.int32, (128, 128), 0)
-    col = lax.broadcasted_iota(jnp.int32, (128, 128), 1)
+    depart(0)
+    mid = product(256, 512, 256, 512)
+    tail = product(512, nv, 0, nv)
+    out_ref[640:FOLD_AT, :] = block(2, 3)
     for pair in range(2):
         upper, lower = block(2 * pair, 2 * pair), block(2 * pair + 1, 2 * pair + 1)
         at = FOLD_AT + 128 * pair
         out_ref[at : at + 128, :] = jnp.where(row <= col, upper, lower)
-    rest = nv - 512
     for j in range(5):
         at = TAIL_AT + TAIL * j
         if j < 4:
@@ -73,6 +75,7 @@
         else:
             out_ref[at : at + TAIL, :] = jnp.zeros((TAIL, 128), F32)
             out_ref[at : at + rest, 0:rest] = tail[:, 512:nv]
+    depart(1)
 
 
 def sweep_kernel(
@@ -340,39 +343,33 @@
         leave(0)
         leave(1)
 
+    prepare()
+
     @pl.when(k == 3)
     def _():
-        prepare()
         backward_step(0)
 
+    def depart(half):
+        main, other = axes[half]
+        for axis in (main, other):
+            relay(half, 0, 0, None, axis, 1)
+            relay(half, 0, 0, None, axis, -1)
+        share(half, 0, 0)
+
     jacobian_copy.wait()
-    form_packed(jacobian[...], error_ref[...] * mask_ref[...].astype(F32), packed_ref)
-    for half in range(2):
-        main, _ = axes[half]
-        relay(half, 0, 0, None, main, 1)
-        relay(half, 0, 0, None, main, -1)
-    for half in range(2):
-        _, other = axes[half]
-        relay(half, 0, 0, None, other, 1)
-        relay(half, 0, 0, None, other, -1)
-    for half in range(2):
-        share(half, 0, 0)
+    form_packed(jacobian[...], error_ref[...] * mask_ref[...].astype(F32), packed_ref, depart)
     own_copy = pltpu.make_async_copy(packed_ref, gathered_ref.at[region], own_sem)
     own_copy.start()
 
-    @pl.when(k != 3)
-    def _():
-        prepare()
-
     events = {
-        3: [(first, 0, -1), (first, 1, -1), (first, 0, 1), (first, 1, 1)],
-        6: [(second, 0, 0, -1), (second, 1, 0, -1), (second, 0, 0, 1), (second, 1, 0, 1)],
-        8: [(opposite, 0), (opposite, 1)],
-        10: [(second, 0, -1, -1), (second, 1, -1, -1), (second, 0, -1, 1), (second, 1, -1, 1)],
-        12: [(second, 0, 1, -1), (second, 1, 1, -1), (second, 0, 1, 1), (second, 1, 1, 1)],
-        14: [(last, 0, 0), (last, 1, 0)],
-        16: [(second, 0, 2, -1), (second, 1, 2, -1), (second, 0, 2, 1), (second, 1, 2, 1)],
-        18: [(last, 0, -1), (last, 1, -1), (last, 0, 1), (last, 1, 1)],
+        5: [(first, 0, -1), (first, 1, -1), (first, 0, 1), (first, 1, 1)],
+        8: [(second, 0, 0, -1), (second, 1, 0, -1), (second, 0, 0, 1), (second, 1, 0, 1)],
+        9: [(opposite, 0), (opposite, 1)],
+        12: [(second, 0, -1, -1), (second, 1, -1, -1), (second, 0, -1, 1), (second, 1, -1, 1)],
+        14: [(second, 0, 1, -1), (second, 1, 1, -1), (second, 0, 1, 1), (second, 1, 1, 1)],
+        15: [(last, 0, 0), (last, 1, 0)],
+        17: [(second, 0, 2, -1), (second, 1, 2, -1), (second, 0, 2, 1), (second, 1, 2, 1)],
+        19: [(last, 0, -1), (last, 1, -1), (last, 0, 1), (last, 1, 1)],
         21: [(last, 0, 2), (last, 1, 2)],
     }
 

time: 118 us -> 115 us (0.975)
  Pallas kernels: 117 us -> 115 us
    pallas_call x1, Pallas kernels: 83.2 us -> 80.4 us  [sweep(): pl.pallas_call(sweep_kernel, out_shape=(jax.ShapeDtypeStruct(chunked, F32...]
where the time goes in v4:
time: 115 us
  Pallas kernels  115 us (100%)
    pallas_call x1, Pallas kernels, sweep(): pl.pallas_call(sweep_kernel, out_shape=(jax.ShapeDtypeStruct(chunked, F32...  80.4 us
    pallas_call x1, Pallas kernels, apply(): pl.pallas_call(apply_kernel, out_shape=(jax.ShapeDtypeStruct((rows, 1, co...  34.2 us

profile of v4, /device:TPU:1, one launch (start us, length us, event | category | flops | bytes accessed | tf_op | source)
XLA Modules:
  0.0 115.3 jit_solution(611770548804956662)
XLA Ops:
  0.6 80.4 %sweep.1 = (f32[8,548,128]{2,1,0:T(8,128)}, f32[8,548,128]{2,1,0:T(8,128)}, f32[32,1224,128]{2,1,0:T(8,128)}) custom-call(f32[548,1,1024]{2,1,0:T(1,128)} %bitcast.9, f32[548,1,1024]{2,1,0:T(1,128)} %bitcast.10, f32[548,1,1024]{2,1,0:T(1,128)} %bitcast.11, f32[548,1,548]{2,1,0:T(1,128)} %bitcast.13, f32[548,1,1024]{2,1,0:T(1,128)} %bitcast.12, ...), custom_call_target="tpu_custom_call" | custom-call | tf_op jit(solution)/shard_map/sweep/pallas_call | solution.py:437
  81.1 34.2 %apply.1 = (f32[548,1,1024]{2,1,0:T(1,128)}, f32[548,1,1024]{2,1,0:T(1,128)}) custom-call(s32[1,1024]{1,0:T(1,128)} %owner_ref.1, f32[8,548,128]{2,1,0:T(8,128)} %get-tuple-element.7.forward_hbm, f32[8,548,128]{2,1,0:T(8,128)} %get-tuple-element.8.swept_hbm, f32[32,1224,128]{2,1,0:T(8,128)} %get-tuple-element.9.gathered_hbm), custom_call_target="tpu_custom_call" | custom-call | tf_op jit(solution)/shard_map/apply/pallas_call | solution.py:611

commit v5 on v4

--- a/solution.py
+++ b/solution.py
@@ -368,9 +368,9 @@
         12: [(second, 0, -1, -1), (second, 1, -1, -1), (second, 0, -1, 1), (second, 1, -1, 1)],
         14: [(second, 0, 1, -1), (second, 1, 1, -1), (second, 0, 1, 1), (second, 1, 1, 1)],
         15: [(last, 0, 0), (last, 1, 0)],
-        17: [(second, 0, 2, -1), (second, 1, 2, -1), (second, 0, 2, 1), (second, 1, 2, 1)],
-        19: [(last, 0, -1), (last, 1, -1), (last, 0, 1), (last, 1, 1)],
-        21: [(last, 0, 2), (last, 1, 2)],
+        16: [(second, 0, 2, -1), (second, 1, 2, -1), (second, 0, 2, 1), (second, 1, 2, 1)],
+        18: [(last, 0, -1), (last, 1, -1), (last, 0, 1), (last, 1, 1)],
+        20: [(last, 0, 2), (last, 1, 2)],
     }
 
     def tick(t, carry):
@@ -553,38 +553,59 @@
                 tall = jnp.concatenate([value, jnp.zeros((128 - rest, 128), F32)], axis=0)
                 put(full, 128 * j, 512, tall.T)
 
-    def one_group(group, carry):
-        at = lax.rem(group, depth)
-        base = (group * wide).astype(F32)
+    def sort(group):
+        base = jnp.asarray(group * wide).astype(F32)
         lane = lax.broadcasted_iota(jnp.int32, (cols, 128), 1).astype(F32) + base
         pick = jnp.concatenate(
             [(slot_col[...] == lane).astype(BF16), (slot_col[...] == lane + 128.0).astype(BF16)], axis=1
         )
         s_high = dot(x_high[...], pick)
         s_low = dot(x_low[...], pick)
-        load_g(group, at).wait()
+        for o in range(each):
+            lanes = slice(128 * (o // 2), 128 * (o // 2) + 128)
+            high = s_high[:, lanes]
+            low = pltpu.roll(s_low[:, lanes], SLOT, 1)
+            mine = left_lanes if o % 2 == 0 else jnp.logical_not(left_lanes)
+            right[o, 0:rows, :] = jnp.where(mine, high, low).astype(BF16)
+            right[o, pad : pad + rows, :] = jnp.where(mine, high, 0.0).astype(BF16)
+
+    def finish(group, outs):
         for pair in range(each // 2):
             lanes = slice(128 * pair, 128 * pair + 128)
-            high = s_high[:, lanes]
-            low = pltpu.roll(s_low[:, lanes], SLOT, 1)
-            outs = []
-            for side in range(2):
-                mine = left_lanes if side == 0 else jnp.logical_not(left_lanes)
-                right[side, 0:rows, :] = jnp.where(mine, high, low).astype(BF16)
-                right[side, pad : pad + rows, :] = jnp.where(mine, high, 0.0).astype(BF16)
-                unpack(packed.at[at, 2 * pair + side], full.at[side])
-                outs.append(dot(full[side], right[side]))
-            even, odd = outs
+            even, odd = outs[2 * pair : 2 * pair + 2]
             answer = jnp.where(left_lanes, even + pltpu.roll(even, SLOT, 1), odd + pltpu.roll(odd, SLOT, 1))
             y_high[group, :, lanes], y_low[group, :, lanes] = split(answer)
 
-        @pl.when(group + depth < groups)
-        def _():
-            load_g(group + depth, at).start()
-
+    def one_group(group, now, later):
+        ahead = group + 1
+        at = lax.rem(ahead, depth)
+        sort(group)
+
+        @pl.when(ahead < groups)
+        def _():
+            load_g(ahead, at).wait()
+
+        outs = []
+        for o in range(each):
+            outs.append(dot(full[now * each + o], right[o]))
+            unpack(packed.at[at, o], full.at[later * each + o])
+        finish(group, outs)
+
+        @pl.when(ahead + depth < groups)
+        def _():
+            load_g(ahead + depth, at).start()
+
+    load_g(0, 0).wait()
+    for o in range(each):
+        unpack(packed.at[0, o], full.at[o])
+    load_g(depth, 0).start()
+
+    def two_groups(i, carry):
+        one_group(2 * i, 0, 1)
+        one_group(2 * i + 1, 1, 0)
         return carry
 
-    lax.fori_loop(0, groups, one_group, 0)
+    lax.fori_loop(0, groups // 2, two_groups, 0)
 
     for c in range(chunks):
         load_s[c].wait()
@@ -621,8 +642,8 @@
             pltpu.VMEM((rows, cols), BF16),
             pltpu.VMEM((cols, 128), F32),
             pltpu.VMEM((groups, wide, cols), BF16),
-            pltpu.VMEM((2, rows, 2 * pad), BF16),
-            pltpu.VMEM((2, 2 * pad, 128), BF16),
+            pltpu.VMEM((8, rows, 2 * pad), BF16),
+            pltpu.VMEM((4, 2 * pad, 128), BF16),
             pltpu.VMEM((groups, rows, wide), BF16),
             pltpu.VMEM((groups, rows, wide), BF16),
             pltpu.SemaphoreType.DMA((2, chunks)),

time: 115 us -> 112 us (0.974)
  Pallas kernels: 115 us -> 111 us
    pallas_call x1, Pallas kernels: 80.4 us -> 78.7 us  [sweep(): pl.pallas_call(sweep_kernel, out_shape=(jax.ShapeDtypeStruct(chunked, F32...]
    pallas_call x1, Pallas kernels: 34.2 us -> 32.5 us  [apply(): pl.pallas_call(apply_kernel, out_shape=(jax.ShapeDtypeStruct((rows, 1, co...]
where the time goes in v5:
time: 112 us
  Pallas kernels  111 us (99%)
    pallas_call x1, Pallas kernels, sweep(): pl.pallas_call(sweep_kernel, out_shape=(jax.ShapeDtypeStruct(chunked, F32...  78.7 us
    pallas_call x1, Pallas kernels, apply(): pl.pallas_call(apply_kernel, out_shape=(jax.ShapeDtypeStruct((rows, 1, co...  32.5 us

profile of v5, /device:TPU:1, one launch (start us, length us, event | category | flops | bytes accessed | tf_op | source)
XLA Modules:
  0.0 112.0 jit_solution(13359334220452639167)
XLA Ops:
  0.6 78.7 %sweep.1 = (f32[8,548,128]{2,1,0:T(8,128)}, f32[8,548,128]{2,1,0:T(8,128)}, f32[32,1224,128]{2,1,0:T(8,128)}) custom-call(f32[548,1,1024]{2,1,0:T(1,128)} %bitcast.9, f32[548,1,1024]{2,1,0:T(1,128)} %bitcast.10, f32[548,1,1024]{2,1,0:T(1,128)} %bitcast.11, f32[548,1,548]{2,1,0:T(1,128)} %bitcast.13, f32[548,1,1024]{2,1,0:T(1,128)} %bitcast.12, ...), custom_call_target="tpu_custom_call" | custom-call | tf_op jit(solution)/shard_map/sweep/pallas_call | solution.py:437
  79.3 32.5 %apply.1 = (f32[548,1,1024]{2,1,0:T(1,128)}, f32[548,1,1024]{2,1,0:T(1,128)}) custom-call(s32[1,1024]{1,0:T(1,128)} %owner_ref.1, f32[8,548,128]{2,1,0:T(8,128)} %get-tuple-element.7.forward_hbm, f32[8,548,128]{2,1,0:T(8,128)} %get-tuple-element.8.swept_hbm, f32[32,1224,128]{2,1,0:T(8,128)} %get-tuple-element.9.gathered_hbm), custom_call_target="tpu_custom_call" | custom-call | tf_op jit(solution)/shard_map/apply/pallas_call | solution.py:632

commit v6 on v5

--- a/solution.py
+++ b/solution.py
@@ -280,12 +280,6 @@
             send_f(2 * c + h).start()
         store_f(one.at[c], c).start()
 
-    def prepare():
-        matrix_copy.wait()
-        value = matrix[...]
-        m_high[...], m_low[...] = split(value)
-        t_high[...], t_low[...] = split(value.T)
-
     def forward_step(s):
         c, h = s // 2, s % 2
 
@@ -343,11 +337,15 @@
         leave(0)
         leave(1)
 
-    prepare()
+    matrix_copy.wait()
+    t_high[...], t_low[...] = split(matrix[...].T)
 
     @pl.when(k == 3)
     def _():
         backward_step(0)
+        backward_step(1)
+
+    m_high[...], m_low[...] = split(matrix[...])
 
     def depart(half):
         main, other = axes[half]
@@ -386,7 +384,7 @@
 
         cb = t - LAG * (3 - k)
 
-        @pl.when((cb >= jnp.where(k == 3, 1, 0)) & (cb < pieces))
+        @pl.when((cb >= jnp.where(k == 3, 2, 0)) & (cb < pieces))
         def _():
             backward_step(cb)
 
@@ -492,11 +490,8 @@
             source.at[c], target.at[:, 0, pl.ds(c * CHUNK, CHUNK)], out_sem.at[which, c]
         )
 
+    load_g(0, 0).start()
     for copy in load_f:
-        copy.start()
-    for at in range(depth):
-        load_g(at, at).start()
-    for copy in load_s:
         copy.start()
 
     owner = owner_ref[...]
@@ -512,7 +507,6 @@
     for group in range(groups):
         place[group] = (jnp.broadcast_to(slot - group * wide, (wide, cols)) == line).astype(BF16)
     right[...] = jnp.zeros_like(right)
-    full[...] = jnp.zeros_like(full)
 
     for c in range(chunks):
         load_f[c].wait()
@@ -596,9 +590,13 @@
             load_g(ahead + depth, at).start()
 
     load_g(0, 0).wait()
+    for at in range(1, depth):
+        load_g(at, at).start()
     for o in range(each):
         unpack(packed.at[0, o], full.at[o])
     load_g(depth, 0).start()
+    for copy in load_s:
+        copy.start()
 
     def two_groups(i, carry):
         one_group(2 * i, 0, 1)

time: 112 us -> 111 us (level)
  no operation moved by 1% of the time
where the time goes in v6:
time: 111 us
  Pallas kernels  110 us (99%)
    pallas_call x1, Pallas kernels, sweep(): pl.pallas_call(sweep_kernel, out_shape=(jax.ShapeDtypeStruct(chunked, F32...  78.4 us
    pallas_call x1, Pallas kernels, apply(): pl.pallas_call(apply_kernel, out_shape=(jax.ShapeDtypeStruct((rows, 1, co...  32 us

profile of v6, /device:TPU:1, one launch (start us, length us, event | category | flops | bytes accessed | tf_op | source)
XLA Modules:
  0.0 111.2 jit_solution(6482417919979786739)
XLA Ops:
  0.6 78.4 %sweep.1 = (f32[8,548,128]{2,1,0:T(8,128)}, f32[8,548,128]{2,1,0:T(8,128)}, f32[32,1224,128]{2,1,0:T(8,128)}) custom-call(f32[548,1,1024]{2,1,0:T(1,128)} %bitcast.9, f32[548,1,1024]{2,1,0:T(1,128)} %bitcast.10, f32[548,1,1024]{2,1,0:T(1,128)} %bitcast.11, f32[548,1,548]{2,1,0:T(1,128)} %bitcast.13, f32[548,1,1024]{2,1,0:T(1,128)} %bitcast.12, ...), custom_call_target="tpu_custom_call" | custom-call | tf_op jit(solution)/shard_map/sweep/pallas_call | solution.py:435
  79.1 32.0 %apply.1 = (f32[548,1,1024]{2,1,0:T(1,128)}, f32[548,1,1024]{2,1,0:T(1,128)}) custom-call(s32[1,1024]{1,0:T(1,128)} %owner_ref.1, f32[8,548,128]{2,1,0:T(8,128)} %get-tuple-element.7.forward_hbm, f32[8,548,128]{2,1,0:T(8,128)} %get-tuple-element.8.swept_hbm, f32[32,1224,128]{2,1,0:T(8,128)} %get-tuple-element.9.gathered_hbm), custom_call_target="tpu_custom_call" | custom-call | tf_op jit(solution)/shard_map/apply/pallas_call | solution.py:630

commit v7 on v6

--- a/solution.py
+++ b/solution.py
@@ -118,9 +118,8 @@
     load(1, 0).start()
     load(2, 0).start()
     jacobian_copy.start()
-    for c in range(1, chunks):
-        for which in range(3):
-            load(which, c).start()
+    for which in range(3):
+        load(which, 1).start()
 
     def store_f(src, c):
         return pltpu.make_async_copy(src, forward_out.at[c], store_sem.at[0, c])
@@ -355,6 +354,9 @@
         share(half, 0, 0)
 
     jacobian_copy.wait()
+    for c in range(2, chunks):
+        for which in range(3):
+            load(which, c).start()
     form_packed(jacobian[...], error_ref[...] * mask_ref[...].astype(F32), packed_ref, depart)
     own_copy = pltpu.make_async_copy(packed_ref, gathered_ref.at[region], own_sem)
     own_copy.start()

time: 111 us -> 111 us (level)
  no operation moved by 1% of the time
where the time goes in v7:
time: 111 us
  Pallas kernels  110 us (99%)
    pallas_call x1, Pallas kernels, sweep(): pl.pallas_call(sweep_kernel, out_shape=(jax.ShapeDtypeStruct(chunked, F32...  78.4 us
    pallas_call x1, Pallas kernels, apply(): pl.pallas_call(apply_kernel, out_shape=(jax.ShapeDtypeStruct((rows, 1, co...  32 us

profile of v7, /device:TPU:1, one launch (start us, length us, event | category | flops | bytes accessed | tf_op | source)
XLA Modules:
  0.0 111.2 jit_solution(3063181609451434751)
XLA Ops:
  0.6 78.4 %sweep.1 = (f32[8,548,128]{2,1,0:T(8,128)}, f32[8,548,128]{2,1,0:T(8,128)}, f32[32,1224,128]{2,1,0:T(8,128)}) custom-call(f32[548,1,1024]{2,1,0:T(1,128)} %bitcast.9, f32[548,1,1024]{2,1,0:T(1,128)} %bitcast.10, f32[548,1,1024]{2,1,0:T(1,128)} %bitcast.11, f32[548,1,548]{2,1,0:T(1,128)} %bitcast.13, f32[548,1,1024]{2,1,0:T(1,128)} %bitcast.12, ...), custom_call_target="tpu_custom_call" | custom-call | tf_op jit(solution)/shard_map/sweep/pallas_call | solution.py:437
  79.1 32.0 %apply.1 = (f32[548,1,1024]{2,1,0:T(1,128)}, f32[548,1,1024]{2,1,0:T(1,128)}) custom-call(s32[1,1024]{1,0:T(1,128)} %owner_ref.1, f32[8,548,128]{2,1,0:T(8,128)} %get-tuple-element.7.forward_hbm, f32[8,548,128]{2,1,0:T(8,128)} %get-tuple-element.8.swept_hbm, f32[32,1224,128]{2,1,0:T(8,128)} %get-tuple-element.9.gathered_hbm), custom_call_target="tpu_custom_call" | custom-call | tf_op jit(solution)/shard_map/apply/pallas_call | solution.py:632
